TPU v7x, 512 devices: a whole 4x4x16 slice. The times are simulated.
512 devices in a mesh: section: 4 (over z_hi), dp: 8 (over x, core), tensor: 16 (over z_lo, y).
Axes of the slice: x: 4, y: 4, z: 16 (z_hi: 4, z_lo: 4; z = z_hi * 4 + z_lo), core: 2. Of those that a mesh axis runs over, the one named last changes fastest.
Arguments:
- hidden: bfloat16 [4, 1024, 28672], P('section', 'tensor', 'dp'), may hold values from -6 to 6
- down_weight: bfloat16 [4, 28672, 8192], P('section', 'dp', 'tensor'), may hold values from -0.03125 to 0.03125
- residual: bfloat16 [4, 1024, 8192], P('section', 'dp', 'tensor'), may hold values from -36 to 36
- norm_gain: float32 [4, 8192], P('section', 'tensor'), may hold values from 0.4 to 1.2
- query_weight: bfloat16 [4, 8192, 4096], P('section', 'tensor', 'dp'), may hold values from -0.0625 to 0.0625
- key_value_weight: bfloat16 [4, 8192, 2048], P('section', 'tensor', 'dp'), may hold values from -0.0625 to 0.0625
Outputs:
- attention: bfloat16 [4, 1024, 4096], P('section', 'tensor', 'dp')
All inputs are finite; a program needn't handle non-finite values.
Results may differ from a plain program's by a relative error of at most 0.04.
Values may be sent and summed in bfloat16 or wider, within the bound.
A program may use at most 64 MiB of HBM per device.

v0:
```python
import jax
import jax.numpy as jnp
from jax import lax
from jax.sharding import PartitionSpec as P

D = 8192
HD = 128


ROPE_BASE = 500000.0
EPSILON = 1e-05


def passed_along(value, axis, steps):
    count = lax.axis_size(axis)
    pairs = [(source, (source + steps) % count) for source in range(count)]
    return lax.ppermute(value, axis, pairs)


def rotate(values, positions):
    half_dim = values.shape[-1] // 2
    frequency = ROPE_BASE ** (-jnp.arange(half_dim, dtype=jnp.float32) * 2.0 / values.shape[-1])
    angles = positions.astype(jnp.float32)[:, None] * frequency[None, :]
    cosine = jnp.cos(angles)[:, None, :]
    sine_part = jnp.sin(angles)[:, None, :]
    front_part = values[..., :half_dim]
    back_part = values[..., half_dim:]
    return jnp.concatenate(
        [front_part * cosine - back_part * sine_part, back_part * cosine + front_part * sine_part],
        axis=-1,
    )


def per_device(hidden, down_weight, residual, norm_gain, query_weight, key_value_weight):
    weight_block = down_weight[0]
    partials = jnp.dot(
        lax.all_gather(hidden[0], "tensor", axis=0, tiled=True),
        weight_block,
        preferred_element_type=jnp.float32,
    )
    summed = lax.psum_scatter(
        partials.astype(jnp.bfloat16), "dp", scatter_dimension=0, tiled=True
    ).astype(jnp.float32)
    boundary = (residual[0].astype(jnp.float32) + summed).astype(jnp.bfloat16)
    gathered = lax.all_gather(boundary, "dp", axis=0, tiled=True)
    arrived = passed_along(gathered, "section", 1)
    values_in = arrived.astype(jnp.float32)
    squares = jnp.sum(values_in * values_in, axis=1)
    scaled = (values_in * norm_gain[0][None, :]).astype(jnp.bfloat16)
    query_sums = jnp.dot(scaled, query_weight[0], preferred_element_type=jnp.float32)
    pair_sums = jnp.dot(scaled, key_value_weight[0], preferred_element_type=jnp.float32)
    token_count = arrived.shape[0]
    own_rows = token_count // lax.axis_size("tensor")
    first_row = lax.axis_index("tensor") * own_rows
    query_sums, pair_sums, squares = (
        lax.psum(query_sums.astype(jnp.bfloat16), "tensor").astype(jnp.float32),
        lax.psum(pair_sums.astype(jnp.bfloat16), "tensor").astype(jnp.float32),
        lax.psum(squares.astype(jnp.bfloat16), "tensor").astype(jnp.float32),
    )
    query_local = lax.dynamic_slice_in_dim(query_sums, first_row, own_rows, 0)
    inverse = lax.rsqrt(squares / D + EPSILON)[:, None]
    positions = jnp.arange(token_count, dtype=jnp.int32)
    own_positions = first_row + jnp.arange(own_rows, dtype=jnp.int32)
    inverse_own = lax.dynamic_slice_in_dim(inverse, first_row, own_rows, 0)
    query_part = query_local * inverse_own
    queries = rotate(query_part.reshape(own_rows, -1, HD), own_positions).astype(jnp.bfloat16)
    pair_rows = (pair_sums * inverse).reshape(token_count, -1, 2, HD)
    key_rows = rotate(pair_rows[:, :, 0], positions).astype(jnp.bfloat16)
    value_rows = pair_rows[:, :, 1].astype(jnp.bfloat16)
    group_count = key_rows.shape[1]
    grouped = queries.reshape(own_rows, group_count, -1, HD)
    scores = jnp.einsum(
        "qgrd,kgd->grqk", grouped, key_rows, preferred_element_type=jnp.float32
    ) * HD ** (-0.5)
    causal = positions[None, :] <= own_positions[:, None]
    scores = jnp.where(causal[None, None], scores, -1e30)
    maximum = jnp.max(scores, axis=-1, keepdims=True)
    weights = jnp.exp(scores - maximum)
    probabilities = (weights / jnp.sum(weights, axis=-1, keepdims=True)).astype(jnp.bfloat16)
    attended = jnp.einsum(
        "grqk,kgd->qgrd", probabilities, value_rows, preferred_element_type=jnp.float32
    ).astype(jnp.bfloat16)
    return attended.reshape(own_rows, -1)[None]


def solution(mesh):
    placed = (
        P("section", "tensor", "dp"),
        P("section", "dp", "tensor"),
        P("section", "dp", "tensor"),
        P("section", "tensor"),
        P("section", "tensor", "dp"),
        P("section", "tensor", "dp"),
    )
    return jax.shard_map(
        per_device,
        mesh=mesh,
        in_specs=placed,
        out_specs=P("section", "tensor", "dp"),
        check_vma=False,
    )
```

profile of v0, /device:TPU:6, one launch (start us, length us, event | category | flops | bytes accessed | tf_op | source)
XLA Modules:
  0.0 486.2 jit_solution(7943351588400073942)
XLA Ops:
  6.5 0.7 all-gather.6.cloned.1.call-update
  7.3 108.6 %all-gather.6.cloned.1.call-done = bf16[1,1024,3584]{2,1,0:T(8,128)(2,1)} async-done(((bf16[1,64,3584]{2,1,0:T(8,128)(2,1)}), bf16[1,1024,3584]{2,1,0:T(8,128)(2,1)}) %all-gather.6.cloned.1.call-update) | async-done | bytes 7340048 | tf_op jit(solution)/shard_map/all_gather | solution.py:37
  115.9 9.1 %fusion.5 = bf16[1024,512]{1,0:T(8,128)(2,1)} fusion(bf16[1,3584,512]{2,1,0:T(8,128)(2,1)} %param.7, bf16[1,1024,3584]{2,1,0:T(8,128)(2,1)} %all-gather.6.cloned.1.call-done), kind=kOutput, calls=%fused_computation.7 | convolution fusion | flops 3758620672 | bytes 12058624 | tf_op jit(solution)/shard_map/dot_general | solution.py:36
  125.0 32.9 %reduce-scatter.2.cloned.1.call-done = bf16[128,512]{1,0:T(8,128)(2,1)} async-done(((bf16[1024,512]{1,0:T(8,128)(2,1)}), bf16[128,512]{1,0:T(8,128)(2,1)}) %reduce-scatter.2.cloned.1.call-update) | async-done | bytes 131088 | tf_op jit(solution)/shard_map/reduce_scatter | solution.py:41
  157.9 1.6 fusion.30
  159.6 32.3 %all-gather.4.cloned.1.call-done = bf16[1024,512]{1,0:T(8,128)(2,1)} async-done(((bf16[128,512]{1,0:T(8,128)(2,1)}), bf16[1024,512]{1,0:T(8,128)(2,1)}) %all-gather.4.cloned.1.call-update) | async-done | bytes 1048592 | tf_op jit(solution)/shard_map/all_gather | solution.py:45
  191.9 7.2 %collective-permute-start = (bf16[1024,512]{1,0:T(8,128)(2,1)}, bf16[1024,512]{1,0:T(8,128)(2,1)S(1)}, u32[]{:S(2)}, u32[]{:S(2)}) collective-permute-start(bf16[1024,512]{1,0:T(8,128)(2,1)} %all-gather.4.cloned.1.call-done), channel_id=1, source_target_pairs={{0,128},{128,256},{256,384},{384,0},{1,129},{129,257},{257,385},{3... | collective-permute-start | bytes 3145736 | tf_op jit(solution)/shard_map/ppermute | solution.py:17
  199.1 55.4 %collective-permute-done = bf16[1024,512]{1,0:T(8,128)(2,1)S(1)} collective-permute-done((bf16[1024,512]{1,0:T(8,128)(2,1)}, bf16[1024,512]{1,0:T(8,128)(2,1)S(1)}, u32[]{:S(2)}, u32[]{:S(2)}) %collective-permute-start) | collective-permute-done | bytes 1048608 | tf_op jit(solution)/shard_map/ppermute | solution.py:17
  254.5 1.3 convolution_convert_fusion.1
  255.7 1.8 convolution_convert_fusion
  257.7 0.2 multiply_cosine_fusion.1
  257.9 0.3 fusion.4
  258.2 79.6 %psum.22 = bf16[1024]{0:T(1024)(128)(2,1)S(1)} all-reduce(bf16[1024]{0:T(1024)(128)(2,1)S(1)} %fusion.4), channel_id=1, replica_groups=mesh['section'=4,'dp'=8,'tensor'=16] {'tensor'}, use_global_device_ids=true, to_apply=%region_3.0 | all-reduce | flops 1024 | bytes 4096 | tf_op jit(solution)/shard_map/psum | solution.py:58
  337.9 133.5 %all-reduce.3.cloned.1.call-done = (bf16[1024,256]{1,0:T(8,128)(2,1)}, bf16[1024,512]{1,0:T(8,128)(2,1)}) async-done(((bf16[1024,256]{1,0:T(8,128)(2,1)}, bf16[1024,512]{1,0:T(8,128)(2,1)}), (bf16[1024,256]{1,0:T(8,128)(2,1)}, bf16[1024,512]{1,0:T(8,128)(2,1)})) %all-reduce.3.cloned.1.call-update) | async-done | bytes 1572880 | tf_op jit(solution)/shard_map/psum | solution.py:57
  471.4 1.2 convert_multiply_fusion.2
  472.7 0.5 reshape.223
  473.2 0.4 slice.26
  473.6 0.5 slice.25
  474.1 0.9 convert_multiply_fusion.3
  475.3 2.4 fusion.33
  477.8 0.5 fusion.40
  478.3 0.3 fusion.13
  478.6 0.4 fusion.12
  479.0 0.7 broadcast_in_dim_reshape.3
  (26 shorter events, 0.7 us)
Async XLA Ops:
  6.5 249.2 %copy-start = (bf16[1,512,512]{2,1,0:T(8,128)(2,1)S(1)}, bf16[1,512,512]{2,1,0:T(8,128)(2,1)}, u32[]{:S(2)}) copy-start(bf16[1,512,512]{2,1,0:T(8,128)(2,1)} %param.10) | copy-start | bytes 1572868
  6.5 109.4 %all-gather.6.cloned.1.call-start = ((), (), s32[]{:S(2)}) async-start(), calls=%async_computation.3 | async-start | bytes 7798784 | tf_op jit(solution)/shard_map/all_gather | solution.py:37
  7.3 150.7 %copy-start.1 = (bf16[1,128,512]{2,1,0:T(8,128)(2,1)S(1)}, bf16[1,128,512]{2,1,0:T(8,128)(2,1)}, u32[]{:S(2)}) copy-start(bf16[1,128,512]{2,1,0:T(8,128)(2,1)} %param.8) | copy-start | bytes 393220
  7.3 247.2 %copy-start.2 = (bf16[1,512,256]{2,1,0:T(8,128)(2,1)S(1)}, bf16[1,512,256]{2,1,0:T(8,128)(2,1)}, u32[]{:S(2)}) copy-start(bf16[1,512,256]{2,1,0:T(8,128)(2,1)} %param.11) | copy-start | bytes 786436
  7.3 247.2 %copy-start.3 = (f32[1,512]{1,0:T(1,128)S(1)}, f32[1,512]{1,0:T(1,128)}, u32[]{:S(2)}) copy-start(f32[1,512]{1,0:T(1,128)} %param.9) | copy-start | bytes 6148
  7.3 150.6 %reduce-scatter.2.cloned.1.call-start = ((), (), s32[]{:S(2)}) async-start(), calls=%async_computation.1 | async-start | bytes 1179648 | tf_op jit(solution)/shard_map/reduce_scatter | solution.py:41
  125.0 66.9 %all-gather.4.cloned.1.call-start = ((), (), s32[]{:S(2)}) async-start(), calls=%async_computation.2 | async-start | bytes 1179648 | tf_op jit(solution)/shard_map/all_gather | solution.py:45
  159.5 311.9 %all-reduce.3.cloned.1.call-start = ((), (), s32[]{:S(2)}) async-start(), calls=%async_computation.4 | async-start | bytes 3145728 | tf_op jit(solution)/shard_map/psum | solution.py:57
  191.9 62.6 %collective-permute-start = (bf16[1024,512]{1,0:T(8,128)(2,1)}, bf16[1024,512]{1,0:T(8,128)(2,1)S(1)}, u32[]{:S(2)}, u32[]{:S(2)}) collective-permute-start(bf16[1024,512]{1,0:T(8,128)(2,1)} %all-gather.4.cloned.1.call-done), channel_id=1, source_target_pairs={{0,128},{128,256},{256,384},{384,0},{1,129},{129,257},{257,385},{3... | collective-permute-start | bytes 3145736 | tf_op jit(solution)/shard_map/ppermute | solution.py:17
Sparse Core Ops, SparseCore 0:
  9.4 106.4 all-gather.5
  125.1 32.7 reduce-scatter.1
  160.1 31.7 all-gather.3
  257.6 213.7 all-reduce.2
where the time goes:
time: 486 us
  waiting for transfers between devices  363 us (75%)
  blocking collectives  79.6 us (16%)
  between operations  13.3 us (3%)
  matrix products  12.9 us (3%)
  starting transfers between devices  7.32 us (2%)
  other arithmetic  7.13 us (1%)
    psum x1, waiting for transfers between devices, per_device(): lax.psum(pair_sums.astype(jnp.bfloat16), 'tensor').astype(jnp.float32)  134 us
    all_gather x1, waiting for transfers between devices, per_device(): lax.all_gather(hidden[0], 'tensor', axis=0, tiled=True)  109 us
    psum x1, blocking collectives, per_device(): lax.psum(squares.astype(jnp.bfloat16), 'tensor').astype(jnp.float32)  79.6 us
    ppermute x1, waiting for transfers between devices, passed_along(): return lax.ppermute(value, axis, pairs)  55.4 us
    reduce_scatter x1, waiting for transfers between devices, per_device(): lax.psum_scatter(partials.astype(jnp.bfloat16), 'dp', scatter_dimension=0...  32.9 us
    all_gather x1, waiting for transfers between devices, per_device(): gathered = lax.all_gather(boundary, 'dp', axis=0, tiled=True)  32.3 us
  transfers between devices with their start and end apart: 5, of which 5 were waited for; matrix products, arithmetic and copies ran while one was open for 0% of the time, Pallas kernels for 0%

commit v1 on v0

v1 whole, which is shorter than its diff:
```python
import jax
import jax.numpy as jnp
from jax import lax
from jax.experimental import pallas as pl
from jax.experimental.pallas import tpu as pltpu
from jax.sharding import PartitionSpec as P

D = 8192
HD = 128
ROPE_BASE = 500000.0
EPSILON = 1e-05

MESH = pl.DeviceIdType.MESH
NZ, NY, ND, NS = 4, 4, 8, 4
NK = 4
ROWS = 16
BF = jnp.bfloat16
F32 = jnp.float32


def kernel(
    hid, w_hbm, wq_hbm, wkv_hbm, res, gain, ctab, stab, out,
    G, W, WP, acc, Pb, R, B, E, U, RY, V, RZ, SQ, SY, SV, SZ, Qb, KV,
    lsem, zsnd, zrcv, ysnd, yrcv, fsnd, frcv, dsnd, drcv, ssnd, srcv, gsnd, grcv,
    usnd, urcv, vsnd, vrcv, qysnd, qyrcv, qzsnd, qzrcv, kzsnd, kzrcv, kysnd, kyrcv,
):
    s = lax.axis_index("section")
    d = lax.axis_index("dp")
    t = lax.axis_index("tensor")
    z, y = t // NY, t % NY
    ff, feats = W.shape
    half = ff // 2
    inner = jnp.logical_and(z > 0, z < NZ - 1)

    def at_z(zz):
        return (s, d, zz * NY + y)

    def at_y(yy):
        return (s, d, z * NY + yy)

    def at_d(dd):
        return (s, dd, t)

    def piece(i):
        return (z, z + 1 - 2 * (z % 2), 2 - z // 2, 3 - 3 * (z // 2))[i]

    def remote(src, dst, snd, rcv, where):
        return pltpu.make_async_remote_copy(
            src_ref=src, dst_ref=dst, send_sem=snd, recv_sem=rcv, device_id=where, device_id_type=MESH
        )

    sent = []

    def send(copy, cond=None):
        if cond is None:
            copy.start()
        else:
            pl.when(cond)(copy.start)
        sent.append((cond, copy))

    local = [
        pltpu.make_async_copy(hid, G.at[:, y, z], lsem.at[0]),
        pltpu.make_async_copy(w_hbm, W, lsem.at[1]),
        pltpu.make_async_copy(wq_hbm, WP.at[:, pl.ds(0, 512)], lsem.at[2]),
        pltpu.make_async_copy(wkv_hbm, WP.at[:, pl.ds(512, 256)], lsem.at[3]),
    ]
    for copy in local:
        copy.start()

    barrier = pltpu.get_barrier_semaphore()
    peers = [at_y((y + j) % NY) for j in range(1, NY)]
    peers += [at_z((z + j) % NZ) for j in range(1, NZ)]
    peers += [at_d((d + j) % ND) for j in range(1, ND)]
    peers += [((s + 1) % NS, d, t), ((s + NS - 1) % NS, d, t)]
    for peer in peers:
        pl.semaphore_signal(barrier, inc=1, device_id=peer, device_id_type=MESH)
    pl.semaphore_wait(barrier, len(peers))
    local[0].wait()

    up, down = (y + 1) % NY, (y + NY - 1) % NY

    def gather_z(k, i):
        zp = piece(i)
        own = G.at[k, y, zp]
        if i == 0:
            send(remote(own, own, zsnd.at[k, 0], zrcv.at[k, zp], at_z(jnp.minimum(z + 1, NZ - 1))), z < NZ - 1)
            send(remote(own, own, zsnd.at[k, 1], zrcv.at[k, zp], at_z(jnp.maximum(z - 1, 0))), z > 0)
        else:
            target = 3 - z if i == 1 else 3 * (z // 2)
            relay = remote(own, own, zsnd.at[k, 1 + i], zrcv.at[k, zp], at_z(target))
            relay.wait_recv()
            send(relay, inner)
        send(remote(own, own, ysnd.at[k, i, 0], yrcv.at[k, i, 0], at_y(up)))
        send(remote(own, own, ysnd.at[k, i, 1], yrcv.at[k, i, 1], at_y(down)))

    def gather_y(k, i):
        zp = piece(i)
        for way, source, target, first in ((0, down, up, 0), (1, up, down, half)):
            whole = G.at[k, source, zp]
            remote(whole, whole, ysnd.at[k, i, way], yrcv.at[k, i, way], at_y(target)).wait_recv()
            part = G.at[k, source, zp, :, pl.ds(first, half)]
            send(remote(part, part, fsnd.at[k, i, way], frcv.at[k, i, way], at_y(target)))

    def gather_end(k):
        far = (y + 2) % NY
        for i in range(NZ):
            zp = piece(i)
            for way, first in ((0, 0), (1, half)):
                part = G.at[k, far, zp, :, pl.ds(first, half)]
                remote(part, part, fsnd.at[k, i, way], frcv.at[k, i, way], at_y(up)).wait_recv()

    def down_project(k):
        depth = ff // 4
        for n in range(4):
            g = G[k, :, :, :, n * depth:(n + 1) * depth].reshape(NY * NZ * ROWS, depth)
            part = jnp.dot(g, W[n * depth:(n + 1) * depth, :], preferred_element_type=F32)
            if n == 0:
                acc[...] = part
            elif n < 3:
                acc[...] += part
            else:
                Pb[k] = (acc[...] + part).astype(BF).reshape(NY, NZ, ROWS, feats)
        for j in range(1, ND):
            dd = (d + j) % ND
            send(remote(Pb.at[k, pl.ds(2 * (dd % 2), 2), dd // 2], R.at[k, j], dsnd.at[k, j], drcv.at[k, j], at_d(dd)))

    def boundary(k):
        total = res[:, k].astype(F32) + Pb[k, pl.ds(2 * (d % 2), 2), d // 2].astype(F32)
        for j in range(1, ND):
            remote(R.at[k, j], R.at[k, j], dsnd.at[k, j], drcv.at[k, j], at_d(d)).wait_recv()
        for j in range(1, ND):
            total = total + R[k, j].astype(F32)
        B[k] = total.astype(BF)
        send(remote(B.at[k], E.at[k, d // 2, d % 2], ssnd.at[k], srcv.at[k], ((s + 1) % NS, d, t)))

    def spread(k):
        own = E.at[k, d // 2, d % 2]
        remote(own, own, ssnd.at[k], srcv.at[k], at_d(d)).wait_recv()
        for j in range(1, ND):
            send(remote(own, own, gsnd.at[k, j], grcv.at[k, j], at_d((d + j) % ND)))

    def project(k):
        for j in range(1, ND):
            dd = (d + ND - j) % ND
            got = E.at[k, dd // 2, dd % 2]
            remote(got, got, gsnd.at[k, j], grcv.at[k, j], at_d(dd)).wait_recv()
        x = E[k].reshape(NY * NZ * ROWS, feats).astype(F32)
        scaled = (x * gain[...]).astype(BF)
        U[k] = jnp.dot(scaled, WP[...], preferred_element_type=F32).astype(BF).reshape(NZ, 2, 2, ROWS, 768)
        SQ[k] = lax.dot_general(
            jnp.ones((8, feats), BF), (x * x).astype(BF), (((1,), (1,)), ((), ())), preferred_element_type=F32
        )
        for j in range(1, NY):
            yy = (y + j) % NY
            send(remote(SQ.at[k], SY.at[k, j], qysnd.at[k, j], qyrcv.at[k, j], at_y(yy)))
            send(remote(U.at[k, :, yy // 2, yy % 2], RY.at[k, j], usnd.at[k, j], urcv.at[k, j], at_y(yy)))

    def sum_y(k):
        for j in range(1, NY):
            remote(SY.at[k, j], SY.at[k, j], qysnd.at[k, j], qyrcv.at[k, j], at_y(y)).wait_recv()
            remote(RY.at[k, j], RY.at[k, j], usnd.at[k, j], urcv.at[k, j], at_y(y)).wait_recv()
        total = U[k, :, y // 2, y % 2].astype(F32)
        squares = SQ[k]
        for j in range(1, NY):
            total = total + RY[k, j].astype(F32)
            squares = squares + SY[k, j]
        V[k] = total.astype(BF)
        SV[k] = squares
        for j in range(1, NZ):
            zz = (z + j) % NZ
            send(remote(SV.at[k], SZ.at[k, j], qzsnd.at[k, j], qzrcv.at[k, j], at_z(zz)))
            send(remote(V.at[k, zz], RZ.at[k, j], vsnd.at[k, j], vrcv.at[k, j], at_z(zz)))

    def sum_z(k):
        for j in range(1, NZ):
            remote(SZ.at[k, j], SZ.at[k, j], qzsnd.at[k, j], qzrcv.at[k, j], at_z(z)).wait_recv()
            remote(RZ.at[k, j], RZ.at[k, j], vsnd.at[k, j], vrcv.at[k, j], at_z(z)).wait_recv()
        total = V[k, z].astype(F32)
        squares = SV[k]
        for j in range(1, NZ):
            total = total + RZ[k, j].astype(F32)
            squares = squares + SZ[k, j]
        tokens = NY * NZ * ROWS
        lane = lax.broadcasted_iota(jnp.int32, (ROWS, tokens), 1)
        row = lax.broadcasted_iota(jnp.int32, (ROWS, tokens), 0)
        row_squares = jnp.broadcast_to(squares[0:1, :], (ROWS, tokens))
        own_squares = jnp.sum(jnp.where(lane == row + t * ROWS, row_squares, 0.0), axis=1, keepdims=True)
        values = total * lax.rsqrt(own_squares / D + EPSILON)
        cosine = ctab[k * ROWS:(k + 1) * ROWS, :]
        sine = stab[k * ROWS:(k + 1) * ROWS, :]

        def rotate(u):
            return (u * cosine + pltpu.roll(u, HD // 2, 1) * sine).astype(BF)

        for h in range(4):
            Qb[h, k * ROWS:(k + 1) * ROWS, :] = rotate(values[:, h * HD:(h + 1) * HD])
        KV[k, y, z, :, 0:HD] = rotate(values[:, 512:640])
        KV[k, y, z, :, HD:2 * HD] = values[:, 640:768].astype(BF)
        own = KV.at[k, y, z]
        for j in range(1, NZ):
            send(remote(own, own, kzsnd.at[k, j], kzrcv.at[k, j], at_z((z + j) % NZ)))

    def pairs_y(k):
        for j in range(1, NZ):
            got = KV.at[k, y, (z + NZ - j) % NZ]
            remote(got, got, kzsnd.at[k, j], kzrcv.at[k, j], at_z(z)).wait_recv()
        own = KV.at[k, y]
        for j in range(1, NY):
            send(remote(own, own, kysnd.at[k, j], kyrcv.at[k, j], at_y((y + j) % NY)))

    def pairs_end(k):
        for j in range(1, NY):
            got = KV.at[k, (y + NY - j) % NY]
            remote(got, got, kysnd.at[k, j], kyrcv.at[k, j], at_y(y)).wait_recv()

    def attend():
        tokens = NK * NY * NZ * ROWS
        queries = Qb[...].reshape(4 * 64, HD)
        keys = KV[:, :, :, :, 0:HD].reshape(tokens, HD)
        values = KV[:, :, :, :, HD:2 * HD].reshape(tokens, HD)
        scores = lax.dot_general(queries, keys, (((1,), (1,)), ((), ())), preferred_element_type=F32) * HD ** (-0.5)
        lane = lax.broadcasted_iota(jnp.int32, (1, tokens), 1)
        key_at = ((lane >> 4) & 3) * 256 + ((lane >> 6) & 3) * 64 + (lane >> 8) * 16 + (lane & 15)
        row = lax.broadcasted_iota(jnp.int32, (256, 1), 0)
        query_at = (row & 63) + t * 64
        scores = jnp.where(key_at <= query_at, scores, -1e30)
        weights = jnp.exp(scores - jnp.max(scores, axis=1, keepdims=True))
        share = (weights / jnp.sum(weights, axis=1, keepdims=True)).astype(BF)
        result = jnp.dot(share, values, preferred_element_type=F32).astype(BF)
        for h in range(4):
            out[:, h * HD:(h + 1) * HD] = result[h * 64:(h + 1) * 64, :]

    def step(f, k):
        if 0 <= k < NK:
            f(k)

    gather_z(0, 0)
    gather_z(1, 0)
    for i in range(1, NZ):
        gather_z(0, i)
    local[1].wait()
    local[2].wait()
    local[3].wait()
    for k in range(NK + 3):
        live = k < NK
        for i in range(NZ):
            if live:
                if i > 0 and k + 1 < NK:
                    gather_z(k + 1, i)
                if i == 0 and 0 < k and k + 1 < NK:
                    gather_z(k + 1, 0)
                gather_y(k, i)
            if i == 0:
                step(sum_y, k - 2)
            if i == 1:
                step(boundary, k - 1)
            if i == 2:
                step(sum_z, k - 2)
            if i == 3:
                step(spread, k - 1)
                step(pairs_y, k - 2)
        if live:
            gather_end(k)
            down_project(k)
        step(project, k - 1)
    for k in range(NK):
        pairs_end(k)
    attend()
    for cond, copy in sent:
        if cond is None:
            copy.wait_send()
        else:
            pl.when(cond)(copy.wait_send)


def per_device(hidden, down_weight, residual, norm_gain, query_weight, key_value_weight):
    own_rows, ff = hidden.shape[1:]
    feats = down_weight.shape[2]
    positions = (lax.axis_index("tensor") * own_rows + jnp.arange(own_rows, dtype=jnp.int32)).astype(F32)
    frequency = ROPE_BASE ** (-jnp.arange(HD // 2, dtype=F32) * 2.0 / HD)
    angles = positions[:, None] * frequency[None, :]
    cosine, sine = jnp.cos(angles), jnp.sin(angles)
    ctab = jnp.concatenate([cosine, cosine], axis=1)
    stab = jnp.concatenate([-sine, sine], axis=1)
    chunk = NY * NZ * ROWS
    dma = pltpu.SemaphoreType.DMA
    vmem = pl.BlockSpec(memory_space=pltpu.VMEM)
    hbm = pl.BlockSpec(memory_space=pl.ANY)
    attended = pl.pallas_call(
        kernel,
        out_shape=jax.ShapeDtypeStruct((own_rows, 512), BF),
        in_specs=[hbm, hbm, hbm, hbm, vmem, vmem, vmem, vmem],
        out_specs=vmem,
        scratch_shapes=[
            pltpu.VMEM((NK, NY, NZ, ROWS, ff), BF),
            pltpu.VMEM((ff, feats), BF),
            pltpu.VMEM((feats, 768), BF),
            pltpu.VMEM((chunk, feats), F32),
            pltpu.VMEM((NK, NY, NZ, ROWS, feats), BF),
            pltpu.VMEM((NK, ND, 2, ROWS, feats), BF),
            pltpu.VMEM((NK, 2, ROWS, feats), BF),
            pltpu.VMEM((NK, NZ, 2, 2, ROWS, feats), BF),
            pltpu.VMEM((NK, NZ, 2, 2, ROWS, 768), BF),
            pltpu.VMEM((NK, NY, NZ, ROWS, 768), BF),
            pltpu.VMEM((NK, NZ, ROWS, 768), BF),
            pltpu.VMEM((NK, NZ, ROWS, 768), BF),
            pltpu.VMEM((NK, 8, chunk), F32),
            pltpu.VMEM((NK, NY, 8, chunk), F32),
            pltpu.VMEM((NK, 8, chunk), F32),
            pltpu.VMEM((NK, NZ, 8, chunk), F32),
            pltpu.VMEM((4, own_rows, HD), BF),
            pltpu.VMEM((NK, NY, NZ, ROWS, 2 * HD), BF),
            dma((4,)),
            dma((NK, 5)), dma((NK, NZ)),
            dma((NK, NZ, 2)), dma((NK, NZ, 2)),
            dma((NK, NZ, 2)), dma((NK, NZ, 2)),
            dma((NK, ND)), dma((NK, ND)),
            dma((NK,)), dma((NK,)),
            dma((NK, ND)), dma((NK, ND)),
            dma((NK, NY)), dma((NK, NY)),
            dma((NK, NZ)), dma((NK, NZ)),
            dma((NK, NY)), dma((NK, NY)),
            dma((NK, NZ)), dma((NK, NZ)),
            dma((NK, NZ)), dma((NK, NZ)),
            dma((NK, NY)), dma((NK, NY)),
        ],
        compiler_params=pltpu.CompilerParams(collective_id=0, has_side_effects=True, vmem_limit_bytes=48 << 20),
    )(
        hidden.reshape(NK, ROWS, ff),
        down_weight[0],
        query_weight[0],
        key_value_weight[0],
        residual.reshape(2, NK, ROWS, feats),
        norm_gain,
        ctab,
        stab,
    )
    return attended[None]


def solution(mesh):
    placed = (
        P("section", "tensor", "dp"),
        P("section", "dp", "tensor"),
        P("section", "dp", "tensor"),
        P("section", "tensor"),
        P("section", "tensor", "dp"),
        P("section", "tensor", "dp"),
    )
    return jax.shard_map(
        per_device,
        mesh=mesh,
        in_specs=placed,
        out_specs=P("section", "tensor", "dp"),
        check_vma=False,
    )
```

time: 486 us -> 161 us (0.33)
  waiting for transfers between devices: 363 us -> 0 us
  Pallas kernels: 0 us -> 151 us
  blocking collectives: 79.6 us -> 0 us
  between operations: 13.3 us -> 0.04 us
  matrix products: 12.9 us -> 0 us
  starting transfers between devices: 7.32 us -> 0 us
  other arithmetic: 7.13 us -> 0.3 us
    pallas_call x0 -> x1, Pallas kernels: none -> 151 us  [per_device(): pl.pallas_call(kernel, out_shape=jax.ShapeDtypeStruct((own_rows, 512), BF...]
    all_gather x2 -> x0, waiting for transfers between devices: 141 us -> none  [the longest x1 109 us: per_device(): lax.all_gather(hidden[0], 'tensor', axis=0, tiled=True)]
    psum x1 -> x0, waiting for transfers between devices: 134 us -> none  [per_device(): lax.psum(pair_sums.astype(jnp.bfloat16), 'tensor').astype(jnp.float32)]
    psum x1 -> x0, blocking collectives: 79.6 us -> none  [per_device(): lax.psum(squares.astype(jnp.bfloat16), 'tensor').astype(jnp.float32)]
    ppermute x1 -> x0, waiting for transfers between devices: 55.4 us -> none  [passed_along(): return lax.ppermute(value, axis, pairs)]
    reduce_scatter x1 -> x0, waiting for transfers between devices: 32.9 us -> none  [per_device(): lax.psum_scatter(partials.astype(jnp.bfloat16), 'dp', scatter_dimension=0...]
    dot_general x5 -> x0, matrix products: 12.9 us -> none  [the longest x1 9.07 us: per_device(): jnp.dot(lax.all_gather(hidden[0], 'tensor', axis=0, tiled=True), weight_b...]
    unnamed x9 -> x13, local copies, waits for them, and re-layouts: 0.05 us -> 7.26 us
  transfers between devices with their start and end apart: 5 -> 0, of which waited for: 5 -> 0; matrix products, arithmetic and copies ran while one was open for 0% -> 0% of each run, Pallas kernels for 0% -> 0%
where the time goes in v1:
time: 161 us; the launch traced here: 159 us
  Pallas kernels  151 us (94%)
  local copies, waits for them, and re-layouts  7.26 us (5%)
    pallas_call x1, Pallas kernels, per_device(): pl.pallas_call(kernel, out_shape=jax.ShapeDtypeStruct((own_rows, 512), BF...  151 us
    unnamed x13, local copies, waits for them, and re-layouts  7.26 us

profile of v1, /device:TPU:6, one launch (start us, length us, event | category | flops | bytes accessed | tf_op | source)
XLA Modules:
  0.0 159.1 jit_solution(1220273849101257442)
XLA Ops:
  0.0 0.2 fusion
  0.2 0.1 pad_maximum_fusion
  0.3 0.0 copy-start
  0.3 2.0 %copy-done = bf16[1,3584,512]{2,1,0:T(8,128)(2,1)S(1)} copy-done((bf16[1,3584,512]{2,1,0:T(8,128)(2,1)S(1)}, bf16[1,3584,512]{2,1,0:T(8,128)(2,1)}, u32[]{:S(2)}) %copy-start) | copy-done | bytes 3670040
  2.4 0.0 copy-start.1
  2.4 1.0 copy-done.1
  3.4 0.0 copy-start.2
  3.4 1.0 copy-done.2
  4.4 0.0 copy-start.3
  4.4 0.9 copy-done.3
  5.4 0.0 copy-start.4
  5.4 0.9 copy-done.4
  6.3 0.0 copy-start.5
  6.3 0.7 copy-done.5
  7.0 151.5 %shard_map.64 = bf16[64,512]{1,0:T(8,128)(2,1)S(1)} custom-call(bf16[4,16,3584]{2,1,0:T(8,128)(2,1)S(1)} %bitcast.8, bf16[3584,512]{1,0:T(8,128)(2,1)S(1)} %bitcast.6, bf16[512,512]{1,0:T(8,128)(2,1)S(1)} %bitcast.7, bf16[512,256]{1,0:T(8,128)(2,1)S(1)} %bitcast.10, bf16[2,4,16,512]{3,2,1,0:T(8,128)(2,1)S(1)} %bitcast.11, f32[1,512]{1,0:T(1,128)S(1)} %copy-done.5, ...), custom_call_target="tpu_custom_call" | custom-call | tf_op jit(solution)/shard_map/pallas_call | solution.py:289
  158.4 0.6 copy.8
  (2 shorter events, 0.0 us)
Async XLA Ops:
  0.3 2.0 %copy-start = (bf16[1,3584,512]{2,1,0:T(8,128)(2,1)S(1)}, bf16[1,3584,512]{2,1,0:T(8,128)(2,1)}, u32[]{:S(2)}) copy-start(bf16[1,3584,512]{2,1,0:T(8,128)(2,1)} %param.7) | copy-start | bytes 11010052
  2.4 1.0 copy-start.1
  3.4 1.0 copy-start.2
  4.4 0.9 copy-start.3
  5.4 0.9 copy-start.4
  6.3 0.7 copy-start.5

commit v2 on v1

--- a/solution.py
+++ b/solution.py
@@ -18,18 +18,42 @@
 F32 = jnp.float32
 
 
+COLS = 22
+ORDER = [
+    ("ry", 1), ("ry", 0), ("gz", 0, 0), ("rf", 1), ("ry", 2), ("rf", 0), ("gz", 1, 0), ("gy", 0, 0),
+    ("gz", 2, 0), ("ry", 3), ("rz", 0, 0), ("gz", 0, 1), ("rz", 1, 0), ("rf", 2), ("gz", 0, 2), ("rz", 0, 1),
+    ("gz", 1, 1), ("rf", 3), ("gy", 1, 0), ("gz", 1, 2), ("gy", 0, 1), ("rz", 2, 0), ("gz", 0, 3), ("gy", 1, 1),
+    ("gz", 2, 1), ("rz", 0, 2), ("gy", 2, 0), ("gz", 1, 3), ("gz", 2, 2), ("gy", 0, 2), ("rz", 3, 0), ("rz", 1, 1),
+    ("rz", 1, 2), ("gy", 0, 3), ("gz", 2, 3), ("gz", 3, 0), ("rz", 0, 3), ("gy", 2, 1), ("ge", 0), ("rz", 2, 1),
+    ("dp", 0), ("gy", 2, 2), ("rz", 1, 3), ("gy", 1, 2), ("gy", 1, 3), ("gy", 2, 3), ("rz", 3, 1), ("gy", 3, 0),
+    ("rz", 3, 2), ("rz", 2, 2), ("gz", 3, 1), ("rz", 2, 3), ("bd", 0), ("ge", 1), ("dp", 1), ("gy", 3, 1),
+    ("gz", 3, 2), ("ge", 2), ("gz", 3, 3), ("dp", 2), ("bd", 1), ("gy", 3, 2), ("gy", 3, 3), ("sp", 0),
+    ("rz", 3, 3), ("sp", 1), ("bd", 2), ("ge", 3), ("dp", 3), ("pp", 0), ("pq", 0), ("sp", 2),
+    ("pp", 1), ("bd", 3), ("pq", 1), ("ky", 0), ("pp", 2), ("sp", 3), ("kz", 0), ("pq", 2),
+    ("ky", 1), ("qy", 0), ("ky", 2), ("pp", 3), ("pq", 3), ("qy", 2), ("py", 0), ("kz", 1),
+    ("ky", 3), ("qy", 1), ("kz", 2), ("py", 1), ("qy", 3), ("kz", 3), ("py", 2), ("qz", 1),
+    ("qz", 0), ("pe", 0), ("qz", 2), ("qz", 3), ("py", 3), ("pe", 2), ("pe", 1), ("at", 0, 2),
+    ("at", 2, 3), ("pe", 3), ("at", 3, 4),
+]
+FLUSH = {("sp", 3): ("dp", 3), ("ky", 3): ("sp", 3), ("pe", 3): ("kz", 3)}
+
+
 def kernel(
-    hid, w_hbm, wq_hbm, wkv_hbm, res, gain, ctab, stab, out,
-    G, W, WP, acc, Pb, R, B, E, U, RY, V, RZ, SQ, SY, SV, SZ, Qb, KV,
-    lsem, zsnd, zrcv, ysnd, yrcv, fsnd, frcv, dsnd, drcv, ssnd, srcv, gsnd, grcv,
-    usnd, urcv, vsnd, vrcv, qysnd, qyrcv, qzsnd, qzrcv, kzsnd, kzrcv, kysnd, kyrcv,
+    hid, w_hbm, wq_hbm, wkv_hbm, res_hbm, gain_hbm, ctab_hbm, stab_hbm, out,
+    res, gain, ctab, stab, peak, mass, mixed,
+    G, W, WP, acc, Pb, R, B, E, XS, UK, UQ, RK, RQ, VK, VQ, ZK, ZQ, SQ, SY, SV, SZ, inv, Qb, KV,
+    lsem, zsnd, zrcv, ysnd, yrcv, fsnd, frcv, bysnd, byrcv, bfsnd, bfrcv, bzsnd, bzrcv, dsnd, drcv, ssnd, srcv, gsnd, grcv,
+    uksnd, ukrcv, uqsnd, uqrcv, vksnd, vkrcv, vqsnd, vqrcv, qysnd, qyrcv, qzsnd, qzrcv, kzsnd, kzrcv, kysnd, kyrcv,
 ):
     s = lax.axis_index("section")
     d = lax.axis_index("dp")
     t = lax.axis_index("tensor")
     z, y = t // NY, t % NY
     ff, feats = W.shape
-    half = ff // 2
+    first_cols = ff * COLS // 28
+    half = first_cols // 2
+    rest = ff - first_cols
+    near, later = pl.ds(0, first_cols), pl.ds(first_cols, rest)
     inner = jnp.logical_and(z > 0, z < NZ - 1)
 
     def at_z(zz):
@@ -63,6 +87,10 @@
         pltpu.make_async_copy(w_hbm, W, lsem.at[1]),
         pltpu.make_async_copy(wq_hbm, WP.at[:, pl.ds(0, 512)], lsem.at[2]),
         pltpu.make_async_copy(wkv_hbm, WP.at[:, pl.ds(512, 256)], lsem.at[3]),
+        pltpu.make_async_copy(res_hbm, res, lsem.at[4]),
+        pltpu.make_async_copy(gain_hbm, gain, lsem.at[5]),
+        pltpu.make_async_copy(ctab_hbm, ctab, lsem.at[6]),
+        pltpu.make_async_copy(stab_hbm, stab, lsem.at[7]),
     ]
     for copy in local:
         copy.start()
@@ -81,7 +109,7 @@
 
     def gather_z(k, i):
         zp = piece(i)
-        own = G.at[k, y, zp]
+        own = G.at[k, y, zp, :, near]
         if i == 0:
             send(remote(own, own, zsnd.at[k, 0], zrcv.at[k, zp], at_z(jnp.minimum(z + 1, NZ - 1))), z < NZ - 1)
             send(remote(own, own, zsnd.at[k, 1], zrcv.at[k, zp], at_z(jnp.maximum(z - 1, 0))), z > 0)
@@ -96,7 +124,7 @@
     def gather_y(k, i):
         zp = piece(i)
         for way, source, target, first in ((0, down, up, 0), (1, up, down, half)):
-            whole = G.at[k, source, zp]
+            whole = G.at[k, source, zp, :, near]
             remote(whole, whole, ysnd.at[k, i, way], yrcv.at[k, i, way], at_y(target)).wait_recv()
             part = G.at[k, source, zp, :, pl.ds(first, half)]
             send(remote(part, part, fsnd.at[k, i, way], frcv.at[k, i, way], at_y(target)))
@@ -108,6 +136,34 @@
             for way, first in ((0, 0), (1, half)):
                 part = G.at[k, far, zp, :, pl.ds(first, half)]
                 remote(part, part, fsnd.at[k, i, way], frcv.at[k, i, way], at_y(up)).wait_recv()
+
+    def rest_y(k):
+        own = G.at[k, y, z, :, later]
+        send(remote(own, own, bysnd.at[k, 0], byrcv.at[k, 0], at_y(up)))
+        send(remote(own, own, bysnd.at[k, 1], byrcv.at[k, 1], at_y(down)))
+
+    def rest_far(k):
+        for way, source, target, first in ((0, down, up, 0), (1, up, down, rest // 2)):
+            whole = G.at[k, source, z, :, later]
+            remote(whole, whole, bysnd.at[k, way], byrcv.at[k, way], at_y(target)).wait_recv()
+            part = G.at[k, source, z, :, pl.ds(first_cols + first, rest // 2)]
+            send(remote(part, part, bfsnd.at[k, way], bfrcv.at[k, way], at_y(target)))
+
+    def rest_z(k, i):
+        zp = piece(i)
+        own = G.at[k, :, zp, :, later]
+        if i == 0:
+            far = (y + 2) % NY
+            for way, first in ((0, 0), (1, rest // 2)):
+                part = G.at[k, far, z, :, pl.ds(first_cols + first, rest // 2)]
+                remote(part, part, bfsnd.at[k, way], bfrcv.at[k, way], at_y(up)).wait_recv()
+            send(remote(own, own, bzsnd.at[k, 0], bzrcv.at[k, zp], at_z(jnp.minimum(z + 1, NZ - 1))), z < NZ - 1)
+            send(remote(own, own, bzsnd.at[k, 1], bzrcv.at[k, zp], at_z(jnp.maximum(z - 1, 0))), z > 0)
+        else:
+            target = 3 - z if i == 1 else 3 * (z // 2)
+            relay = remote(own, own, bzsnd.at[k, 1 + i], bzrcv.at[k, zp], at_z(target))
+            relay.wait_recv()
+            send(relay, inner)
 
     def down_project(k):
         depth = ff // 4
@@ -139,66 +195,90 @@
         for j in range(1, ND):
             send(remote(own, own, gsnd.at[k, j], grcv.at[k, j], at_d((d + j) % ND)))
 
-    def project(k):
+    def project_pairs(k):
         for j in range(1, ND):
             dd = (d + ND - j) % ND
             got = E.at[k, dd // 2, dd % 2]
             remote(got, got, gsnd.at[k, j], grcv.at[k, j], at_d(dd)).wait_recv()
         x = E[k].reshape(NY * NZ * ROWS, feats).astype(F32)
         scaled = (x * gain[...]).astype(BF)
-        U[k] = jnp.dot(scaled, WP[...], preferred_element_type=F32).astype(BF).reshape(NZ, 2, 2, ROWS, 768)
+        XS[k] = scaled
+        UK[k] = jnp.dot(scaled, WP[:, 512:768], preferred_element_type=F32).astype(BF).reshape(NZ, 2, 2, ROWS, 256)
         SQ[k] = lax.dot_general(
             jnp.ones((8, feats), BF), (x * x).astype(BF), (((1,), (1,)), ((), ())), preferred_element_type=F32
         )
         for j in range(1, NY):
             yy = (y + j) % NY
+            send(remote(UK.at[k, :, yy // 2, yy % 2], RK.at[k, j], uksnd.at[k, j], ukrcv.at[k, j], at_y(yy)))
             send(remote(SQ.at[k], SY.at[k, j], qysnd.at[k, j], qyrcv.at[k, j], at_y(yy)))
-            send(remote(U.at[k, :, yy // 2, yy % 2], RY.at[k, j], usnd.at[k, j], urcv.at[k, j], at_y(yy)))
-
-    def sum_y(k):
-        for j in range(1, NY):
+
+    def project_queries(k):
+        UQ[k] = jnp.dot(XS[k], WP[:, 0:512], preferred_element_type=F32).astype(BF).reshape(NZ, 2, 2, ROWS, 512)
+        for j in range(1, NY):
+            yy = (y + j) % NY
+            send(remote(UQ.at[k, :, yy // 2, yy % 2], RQ.at[k, j], uqsnd.at[k, j], uqrcv.at[k, j], at_y(yy)))
+
+    def sum_pairs_y(k):
+        for j in range(1, NY):
+            remote(RK.at[k, j], RK.at[k, j], uksnd.at[k, j], ukrcv.at[k, j], at_y(y)).wait_recv()
             remote(SY.at[k, j], SY.at[k, j], qysnd.at[k, j], qyrcv.at[k, j], at_y(y)).wait_recv()
-            remote(RY.at[k, j], RY.at[k, j], usnd.at[k, j], urcv.at[k, j], at_y(y)).wait_recv()
-        total = U[k, :, y // 2, y % 2].astype(F32)
+        total = UK[k, :, y // 2, y % 2].astype(F32)
         squares = SQ[k]
         for j in range(1, NY):
-            total = total + RY[k, j].astype(F32)
+            total = total + RK[k, j].astype(F32)
             squares = squares + SY[k, j]
-        V[k] = total.astype(BF)
+        VK[k] = total.astype(BF)
         SV[k] = squares
         for j in range(1, NZ):
             zz = (z + j) % NZ
+            send(remote(VK.at[k, zz], ZK.at[k, j], vksnd.at[k, j], vkrcv.at[k, j], at_z(zz)))
             send(remote(SV.at[k], SZ.at[k, j], qzsnd.at[k, j], qzrcv.at[k, j], at_z(zz)))
-            send(remote(V.at[k, zz], RZ.at[k, j], vsnd.at[k, j], vrcv.at[k, j], at_z(zz)))
-
-    def sum_z(k):
-        for j in range(1, NZ):
+
+    def sum_queries_y(k):
+        for j in range(1, NY):
+            remote(RQ.at[k, j], RQ.at[k, j], uqsnd.at[k, j], uqrcv.at[k, j], at_y(y)).wait_recv()
+        total = UQ[k, :, y // 2, y % 2].astype(F32)
+        for j in range(1, NY):
+            total = total + RQ[k, j].astype(F32)
+        VQ[k] = total.astype(BF)
+        for j in range(1, NZ):
+            zz = (z + j) % NZ
+            send(remote(VQ.at[k, zz], ZQ.at[k, j], vqsnd.at[k, j], vqrcv.at[k, j], at_z(zz)))
+
+    def rotate(u, k):
+        rows = pl.ds(k * ROWS, ROWS)
+        return (u * ctab[rows, :] + pltpu.roll(u, HD // 2, 1) * stab[rows, :]).astype(BF)
+
+    def sum_pairs_z(k):
+        for j in range(1, NZ):
+            remote(ZK.at[k, j], ZK.at[k, j], vksnd.at[k, j], vkrcv.at[k, j], at_z(z)).wait_recv()
             remote(SZ.at[k, j], SZ.at[k, j], qzsnd.at[k, j], qzrcv.at[k, j], at_z(z)).wait_recv()
-            remote(RZ.at[k, j], RZ.at[k, j], vsnd.at[k, j], vrcv.at[k, j], at_z(z)).wait_recv()
-        total = V[k, z].astype(F32)
+        total = VK[k, z].astype(F32)
         squares = SV[k]
         for j in range(1, NZ):
-            total = total + RZ[k, j].astype(F32)
+            total = total + ZK[k, j].astype(F32)
             squares = squares + SZ[k, j]
         tokens = NY * NZ * ROWS
         lane = lax.broadcasted_iota(jnp.int32, (ROWS, tokens), 1)
         row = lax.broadcasted_iota(jnp.int32, (ROWS, tokens), 0)
         row_squares = jnp.broadcast_to(squares[0:1, :], (ROWS, tokens))
         own_squares = jnp.sum(jnp.where(lane == row + t * ROWS, row_squares, 0.0), axis=1, keepdims=True)
-        values = total * lax.rsqrt(own_squares / D + EPSILON)
-        cosine = ctab[k * ROWS:(k + 1) * ROWS, :]
-        sine = stab[k * ROWS:(k + 1) * ROWS, :]
-
-        def rotate(u):
-            return (u * cosine + pltpu.roll(u, HD // 2, 1) * sine).astype(BF)
-
+        inverse = lax.rsqrt(own_squares / D + EPSILON)
+        inv[k] = jnp.broadcast_to(inverse, (ROWS, HD))
+        KV[k, y, z, :, 0:HD] = rotate(total[:, 0:HD] * inverse, k)
+        KV[k, y, z, :, HD:2 * HD] = (total[:, HD:2 * HD] * inverse).astype(BF)
+        own = KV.at[k, y, z]
+        for j in range(1, NZ):
+            send(remote(own, own, kzsnd.at[k, j], kzrcv.at[k, j], at_z((z + j) % NZ)))
+
+    def sum_queries_z(k):
+        for j in range(1, NZ):
+            remote(ZQ.at[k, j], ZQ.at[k, j], vqsnd.at[k, j], vqrcv.at[k, j], at_z(z)).wait_recv()
+        total = VQ[k, z].astype(F32)
+        for j in range(1, NZ):
+            total = total + ZQ[k, j].astype(F32)
         for h in range(4):
-            Qb[h, k * ROWS:(k + 1) * ROWS, :] = rotate(values[:, h * HD:(h + 1) * HD])
-        KV[k, y, z, :, 0:HD] = rotate(values[:, 512:640])
-        KV[k, y, z, :, HD:2 * HD] = values[:, 640:768].astype(BF)
-        own = KV.at[k, y, z]
-        for j in range(1, NZ):
-            send(remote(own, own, kzsnd.at[k, j], kzrcv.at[k, j], at_z((z + j) % NZ)))
+            Qb[h, k * ROWS:(k + 1) * ROWS, :] = rotate(total[:, h * HD:(h + 1) * HD] * inv[k], k)
 
     def pairs_y(k):
         for j in range(1, NZ):
@@ -213,64 +293,64 @@
             got = KV.at[k, (y + NY - j) % NY]
             remote(got, got, kysnd.at[k, j], kyrcv.at[k, j], at_y(y)).wait_recv()
 
-    def attend():
-        tokens = NK * NY * NZ * ROWS
+    def attend(first, last):
+        tokens = (last - first) * NY * NZ * ROWS
         queries = Qb[...].reshape(4 * 64, HD)
-        keys = KV[:, :, :, :, 0:HD].reshape(tokens, HD)
-        values = KV[:, :, :, :, HD:2 * HD].reshape(tokens, HD)
+        keys = KV[first:last, :, :, :, 0:HD].reshape(tokens, HD)
+        values = KV[first:last, :, :, :, HD:2 * HD].reshape(tokens, HD)
         scores = lax.dot_general(queries, keys, (((1,), (1,)), ((), ())), preferred_element_type=F32) * HD ** (-0.5)
-        lane = lax.broadcasted_iota(jnp.int32, (1, tokens), 1)
+        lane = lax.broadcasted_iota(jnp.int32, (1, tokens), 1) + first * NY * NZ * ROWS
         key_at = ((lane >> 4) & 3) * 256 + ((lane >> 6) & 3) * 64 + (lane >> 8) * 16 + (lane & 15)
         row = lax.broadcasted_iota(jnp.int32, (256, 1), 0)
         query_at = (row & 63) + t * 64
         scores = jnp.where(key_at <= query_at, scores, -1e30)
-        weights = jnp.exp(scores - jnp.max(scores, axis=1, keepdims=True))
-        share = (weights / jnp.sum(weights, axis=1, keepdims=True)).astype(BF)
-        result = jnp.dot(share, values, preferred_element_type=F32).astype(BF)
-        for h in range(4):
-            out[:, h * HD:(h + 1) * HD] = result[h * 64:(h + 1) * 64, :]
-
-    def step(f, k):
-        if 0 <= k < NK:
-            f(k)
-
-    gather_z(0, 0)
-    gather_z(1, 0)
-    for i in range(1, NZ):
-        gather_z(0, i)
-    local[1].wait()
-    local[2].wait()
-    local[3].wait()
-    for k in range(NK + 3):
-        live = k < NK
-        for i in range(NZ):
-            if live:
-                if i > 0 and k + 1 < NK:
-                    gather_z(k + 1, i)
-                if i == 0 and 0 < k and k + 1 < NK:
-                    gather_z(k + 1, 0)
-                gather_y(k, i)
-            if i == 0:
-                step(sum_y, k - 2)
-            if i == 1:
-                step(boundary, k - 1)
-            if i == 2:
-                step(sum_z, k - 2)
-            if i == 3:
-                step(spread, k - 1)
-                step(pairs_y, k - 2)
-        if live:
-            gather_end(k)
-            down_project(k)
-        step(project, k - 1)
-    for k in range(NK):
-        pairs_end(k)
-    attend()
-    for cond, copy in sent:
-        if cond is None:
-            copy.wait_send()
+        top = jnp.max(scores, axis=1, keepdims=True)
+        if first > 0:
+            top = jnp.maximum(top, peak[...])
+        weights = jnp.exp(scores - top)
+        total = jnp.sum(weights, axis=1, keepdims=True)
+        result = jnp.dot(weights.astype(BF), values, preferred_element_type=F32)
+        if first > 0:
+            fade = jnp.exp(peak[...] - top)
+            total = total + mass[...] * fade
+            result = result + mixed[...] * fade
+        if last < NK:
+            peak[...] = top
+            mass[...] = total
+            mixed[...] = result
         else:
-            pl.when(cond)(copy.wait_send)
+            result = (result / total).astype(BF)
+            for h in range(4):
+                out[:, h * HD:(h + 1) * HD] = result[h * 64:(h + 1) * 64, :]
+
+    def flush(count):
+        for cond, copy in sent[:count]:
+            if cond is None:
+                copy.wait_send()
+            else:
+                pl.when(cond)(copy.wait_send)
+        del sent[:count]
+
+    steps = dict(
+        gz=gather_z, gy=gather_y, ge=gather_end, ry=rest_y, rf=rest_far, rz=rest_z, dp=down_project, bd=boundary,
+        sp=spread, pp=project_pairs, pq=project_queries, ky=sum_pairs_y, qy=sum_queries_y, kz=sum_pairs_z,
+        qz=sum_queries_z, py=pairs_y, pe=pairs_end, at=attend,
+    )
+    waited = False
+    marks = {}
+    for name, *at in ORDER:
+        token = (name, *at)
+        if name == "dp" and not waited:
+            waited = True
+            for copy in local[1:]:
+                copy.wait()
+        if token in FLUSH:
+            count = marks[FLUSH[token]] - marks.get("done", 0)
+            marks["done"] = marks[FLUSH[token]]
+            flush(count)
+        marks[token] = marks.get("done", 0) + len(sent)
+        steps[name](*at)
+    flush(len(sent))
 
 
 def per_device(hidden, down_weight, residual, norm_gain, query_weight, key_value_weight):
@@ -285,13 +365,20 @@
     chunk = NY * NZ * ROWS
     dma = pltpu.SemaphoreType.DMA
     vmem = pl.BlockSpec(memory_space=pltpu.VMEM)
-    hbm = pl.BlockSpec(memory_space=pl.ANY)
+    hbm = pl.BlockSpec(memory_space=pltpu.HBM)
     attended = pl.pallas_call(
         kernel,
         out_shape=jax.ShapeDtypeStruct((own_rows, 512), BF),
-        in_specs=[hbm, hbm, hbm, hbm, vmem, vmem, vmem, vmem],
+        in_specs=[hbm] * 8,
         out_specs=vmem,
         scratch_shapes=[
+            pltpu.VMEM((2, NK, ROWS, feats), BF),
+            pltpu.VMEM((1, feats), F32),
+            pltpu.VMEM((own_rows, HD), F32),
+            pltpu.VMEM((own_rows, HD), F32),
+            pltpu.VMEM((4 * own_rows, 1), F32),
+            pltpu.VMEM((4 * own_rows, 1), F32),
+            pltpu.VMEM((4 * own_rows, HD), F32),
             pltpu.VMEM((NK, NY, NZ, ROWS, ff), BF),
             pltpu.VMEM((ff, feats), BF),
             pltpu.VMEM((feats, 768), BF),
@@ -300,31 +387,42 @@
             pltpu.VMEM((NK, ND, 2, ROWS, feats), BF),
             pltpu.VMEM((NK, 2, ROWS, feats), BF),
             pltpu.VMEM((NK, NZ, 2, 2, ROWS, feats), BF),
-            pltpu.VMEM((NK, NZ, 2, 2, ROWS, 768), BF),
-            pltpu.VMEM((NK, NY, NZ, ROWS, 768), BF),
-            pltpu.VMEM((NK, NZ, ROWS, 768), BF),
-            pltpu.VMEM((NK, NZ, ROWS, 768), BF),
+            pltpu.VMEM((NK, chunk, feats), BF),
+            pltpu.VMEM((NK, NZ, 2, 2, ROWS, 256), BF),
+            pltpu.VMEM((NK, NZ, 2, 2, ROWS, 512), BF),
+            pltpu.VMEM((NK, NY, NZ, ROWS, 256), BF),
+            pltpu.VMEM((NK, NY, NZ, ROWS, 512), BF),
+            pltpu.VMEM((NK, NZ, ROWS, 256), BF),
+            pltpu.VMEM((NK, NZ, ROWS, 512), BF),
+            pltpu.VMEM((NK, NZ, ROWS, 256), BF),
+            pltpu.VMEM((NK, NZ, ROWS, 512), BF),
             pltpu.VMEM((NK, 8, chunk), F32),
             pltpu.VMEM((NK, NY, 8, chunk), F32),
             pltpu.VMEM((NK, 8, chunk), F32),
             pltpu.VMEM((NK, NZ, 8, chunk), F32),
+            pltpu.VMEM((NK, ROWS, HD), F32),
             pltpu.VMEM((4, own_rows, HD), BF),
             pltpu.VMEM((NK, NY, NZ, ROWS, 2 * HD), BF),
-            dma((4,)),
+            dma((8,)),
             dma((NK, 5)), dma((NK, NZ)),
             dma((NK, NZ, 2)), dma((NK, NZ, 2)),
             dma((NK, NZ, 2)), dma((NK, NZ, 2)),
+            dma((NK, 2)), dma((NK, 2)),
+            dma((NK, 2)), dma((NK, 2)),
+            dma((NK, 5)), dma((NK, NZ)),
             dma((NK, ND)), dma((NK, ND)),
             dma((NK,)), dma((NK,)),
             dma((NK, ND)), dma((NK, ND)),
             dma((NK, NY)), dma((NK, NY)),
+            dma((NK, NY)), dma((NK, NY)),
+            dma((NK, NZ)), dma((NK, NZ)),
             dma((NK, NZ)), dma((NK, NZ)),
             dma((NK, NY)), dma((NK, NY)),
             dma((NK, NZ)), dma((NK, NZ)),
             dma((NK, NZ)), dma((NK, NZ)),
             dma((NK, NY)), dma((NK, NY)),
         ],
-        compiler_params=pltpu.CompilerParams(collective_id=0, has_side_effects=True, vmem_limit_bytes=48 << 20),
+        compiler_params=pltpu.CompilerParams(collective_id=0, has_side_effects=True, vmem_limit_bytes=62 << 20),
     )(
         hidden.reshape(NK, ROWS, ff),
         down_weight[0],

time: 161 us -> 119 us (0.74)
  Pallas kernels: 151 us -> 115 us
  local copies, waits for them, and re-layouts: 7.26 us -> 1.47 us
    pallas_call x1, Pallas kernels: 151 us -> 115 us  [per_device(): pl.pallas_call(kernel, out_shape=jax.ShapeDtypeStruct((own_rows, 512), BF...]
    unnamed x13 -> x1, local copies, waits for them, and re-layouts: 7.26 us -> 1.47 us
where the time goes in v2:
time: 119 us; the launch traced here: 117 us
  Pallas kernels  115 us (97%)
  local copies, waits for them, and re-layouts  1.47 us (1%)
    pallas_call x1, Pallas kernels, per_device(): pl.pallas_call(kernel, out_shape=jax.ShapeDtypeStruct((own_rows, 512), BF...  115 us

profile of v2, /device:TPU:6, one launch (start us, length us, event | category | flops | bytes accessed | tf_op | source)
XLA Modules:
  0.0 117.0 jit_solution(12356722202702119451)
XLA Ops:
  0.0 0.2 fusion
  0.2 0.7 pad_maximum_fusion
  0.9 114.6 %shard_map.64 = bf16[64,512]{1,0:T(8,128)(2,1)} custom-call(bf16[4,16,3584]{2,1,0:T(8,128)(2,1)} %bitcast.8, bf16[3584,512]{1,0:T(8,128)(2,1)} %bitcast.6, bf16[512,512]{1,0:T(8,128)(2,1)} %bitcast.7, bf16[512,256]{1,0:T(8,128)(2,1)} %bitcast.10, bf16[2,4,16,512]{3,2,1,0:T(8,128)(2,1)} %bitcast.11, f32[1,512]{1,0:T(1,128)} %gain_hbm.1, ...), custom_call_target="tpu_custom_call" | custom-call | tf_op jit(solution)/shard_map/pallas_call | solution.py:369
  115.5 1.5 %copy.8 = bf16[1,64,512]{2,1,0:T(8,128)(2,1)} copy(bf16[1,64,512]{2,1,0:T(8,128)(2,1)} %bitcast.9) | data formatting | bytes 131072
  (2 shorter events, 0.0 us)

commit v3 on v2

v3 whole, which is shorter than its diff:
```python
import jax
import jax.numpy as jnp
from jax import lax
from jax.experimental import pallas as pl
from jax.experimental.pallas import tpu as pltpu
from jax.sharding import PartitionSpec as P

D = 8192
HD = 128
ROPE_BASE = 500000.0
EPSILON = 1e-05

MESH = pl.DeviceIdType.MESH
NZ, NY, ND, NS = 4, 4, 8, 4
NK = 4
ROWS = 16
BF = jnp.bfloat16
F32 = jnp.float32


COLS = 24
ORDER = [
    ("ry", 1), ("ry", 0), ("ry", 3), ("gz", 0, 0), ("gz", 1, 0), ("rf", 3), ("rf", 1), ("rf", 0),
    ("ry", 2), ("gz", 0, 1), ("gz", 1, 1), ("gz", 2, 0), ("gz", 0, 2), ("rz", 1, 0), ("rz", 0, 0), ("gy", 0, 0),
    ("rf", 2), ("gz", 0, 3), ("gy", 2, 0), ("gz", 2, 1), ("gy", 0, 1), ("rz", 1, 1), ("gz", 1, 2), ("gy", 0, 2),
    ("rz", 2, 0), ("gy", 1, 0), ("gz", 1, 3), ("rz", 0, 1), ("gy", 0, 3), ("rz", 0, 2), ("rz", 3, 0), ("gz", 3, 0),
    ("gz", 2, 2), ("rz", 0, 3), ("gz", 2, 3), ("rz", 1, 2), ("rz", 2, 1), ("gy", 1, 1), ("rz", 1, 3), ("ge", 0),
    ("dp", 0), ("gy", 1, 2), ("rz", 2, 2), ("gy", 1, 3), ("rz", 3, 1), ("gy", 2, 1), ("gz", 3, 1), ("rz", 3, 2),
    ("gy", 2, 2), ("bd", 0), ("gy", 2, 3), ("gz", 3, 2), ("ge", 1), ("rz", 2, 3), ("dp", 1), ("gy", 3, 0),
    ("gz", 3, 3), ("sp", 0), ("gy", 3, 1), ("ge", 2), ("bd", 1), ("dp", 2), ("rz", 3, 3), ("gy", 3, 2),
    ("gy", 3, 3), ("sp", 1), ("bd", 2), ("ge", 3), ("dp", 3), ("pp", 0), ("pq", 0), ("sp", 2),
    ("pp", 1), ("pq", 1), ("bd", 3), ("pp", 2), ("pq", 2), ("sp", 3), ("ky", 1), ("ky", 0),
    ("qy", 1), ("pp", 3), ("ky", 2), ("pq", 3), ("kz", 0), ("qy", 0), ("ky", 3), ("kz", 2),
    ("kz", 1), ("py", 0), ("qy", 2), ("qz", 0), ("qz", 1), ("kz", 3), ("py", 2), ("qy", 3),
    ("py", 1), ("py", 3), ("qz", 2), ("pe", 2), ("pe", 0), ("pe", 1), ("qz", 3), ("at", 0, 2),
    ("at", 2, 3), ("pe", 3), ("at", 3, 4),
]
LOADED = min(ORDER.index(("dp", k)) for k in range(NK))
GATHERED = ORDER.index(("sp", 3))
LEFT = ORDER.index(("at", 3, 4)) - 1


def kernel(
    hid, w_hbm, wq_hbm, wkv_hbm, res_hbm, gain_hbm, ctab_hbm, stab_hbm, out,
    res, gain, ctab, stab, peak, mass, mixed,
    G, W, WP, acc, Pb, R, B, E, XS, UK, UQ, RK, RQ, VK, VQ, ZK, ZQ, SQ, SY, SV, SZ, inv, Qb, KV,
    lsem, zsnd, osnd,
    zrcv, yrcv, frcv, byrcv, bfrcv, bzrcv,
    drcv, srcv, grcv, ukrcv, uqrcv, vkrcv,
    vqrcv, qyrcv, qzrcv, kzrcv, kyrcv,
):
    s = lax.axis_index("section")
    d = lax.axis_index("dp")
    t = lax.axis_index("tensor")
    z, y = t // NY, t % NY
    ff, feats = W.shape
    first_cols = ff * COLS // 28
    half = first_cols // 2
    rest = ff - first_cols
    near, later = pl.ds(0, first_cols), pl.ds(first_cols, rest)
    inner = jnp.logical_and(z > 0, z < NZ - 1)

    def at_z(zz):
        return (s, d, zz * NY + y)

    def at_y(yy):
        return (s, d, z * NY + yy)

    def at_d(dd):
        return (s, dd, t)

    def piece(i):
        return (z, z + 1 - 2 * (z % 2), 2 - z // 2, 3 - 3 * (z // 2))[i]

    def remote(src, dst, snd, rcv, where):
        return pltpu.make_async_remote_copy(
            src_ref=src, dst_ref=dst, send_sem=snd, recv_sem=rcv, device_id=where, device_id_type=MESH
        )

    def send(copy, cond=None):
        if cond is None:
            copy.start()
        else:
            pl.when(cond)(copy.start)

    def drain(ref, sem):
        pltpu.make_async_copy(ref, ref, sem).wait()

    local = [
        pltpu.make_async_copy(hid, G.at[:, y, z], lsem.at[0]),
        pltpu.make_async_copy(w_hbm, W, lsem.at[1]),
        pltpu.make_async_copy(wq_hbm, WP.at[:, pl.ds(0, 512)], lsem.at[2]),
        pltpu.make_async_copy(wkv_hbm, WP.at[:, pl.ds(512, 256)], lsem.at[3]),
        pltpu.make_async_copy(res_hbm, res, lsem.at[4]),
        pltpu.make_async_copy(gain_hbm, gain, lsem.at[5]),
        pltpu.make_async_copy(ctab_hbm, ctab, lsem.at[6]),
        pltpu.make_async_copy(stab_hbm, stab, lsem.at[7]),
    ]
    for copy in local:
        copy.start()

    barrier = pltpu.get_barrier_semaphore()
    peers = [at_y((y + j) % NY) for j in range(1, NY)]
    peers += [at_z((z + j) % NZ) for j in range(1, NZ)]
    peers += [at_d((d + j) % ND) for j in range(1, ND)]
    peers += [((s + 1) % NS, d, t), ((s + NS - 1) % NS, d, t)]
    for peer in peers:
        pl.semaphore_signal(barrier, inc=1, device_id=peer, device_id_type=MESH)
    pl.semaphore_wait(barrier, len(peers))
    local[0].wait()

    up, down = (y + 1) % NY, (y + NY - 1) % NY

    def gather_z(k, i):
        zp = piece(i)
        own = G.at[k, y, zp, :, near]
        if i == 0:
            send(remote(own, own, zsnd.at[0], zrcv.at[k, zp], at_z(jnp.minimum(z + 1, NZ - 1))), z < NZ - 1)
            send(remote(own, own, zsnd.at[0], zrcv.at[k, zp], at_z(jnp.maximum(z - 1, 0))), z > 0)
        else:
            target = 3 - z if i == 1 else 3 * (z // 2)
            relay = remote(own, own, zsnd.at[1], zrcv.at[k, zp], at_z(target))
            relay.wait_recv()
            send(relay, inner)
        send(remote(own, own, osnd.at[0], yrcv.at[k, i, 0], at_y(up)))
        send(remote(own, own, osnd.at[0], yrcv.at[k, i, 1], at_y(down)))

    def gather_y(k, i):
        zp = piece(i)
        for way, source, target, first in ((0, down, up, 0), (1, up, down, half)):
            whole = G.at[k, source, zp, :, near]
            drain(whole, yrcv.at[k, i, way])
            part = G.at[k, source, zp, :, pl.ds(first, half)]
            send(remote(part, part, osnd.at[1], frcv.at[k], at_y(target)))

    def gather_end(k):
        drain(G.at[k, (y + 2) % NY, :, :, near], frcv.at[k])

    def rest_y(k):
        own = G.at[k, y, z, :, later]
        send(remote(own, own, osnd.at[2], byrcv.at[k, 0], at_y(up)))
        send(remote(own, own, osnd.at[2], byrcv.at[k, 1], at_y(down)))

    def rest_far(k):
        for way, source, target, first in ((0, down, up, 0), (1, up, down, rest // 2)):
            whole = G.at[k, source, z, :, later]
            drain(whole, byrcv.at[k, way])
            part = G.at[k, source, z, :, pl.ds(first_cols + first, rest // 2)]
            send(remote(part, part, osnd.at[3], bfrcv.at[k], at_y(target)))

    def rest_z(k, i):
        zp = piece(i)
        own = G.at[k, :, zp, :, later]
        if i == 0:
            drain(G.at[k, (y + 2) % NY, z, :, later], bfrcv.at[k])
            send(remote(own, own, zsnd.at[2], bzrcv.at[k, zp], at_z(jnp.minimum(z + 1, NZ - 1))), z < NZ - 1)
            send(remote(own, own, zsnd.at[2], bzrcv.at[k, zp], at_z(jnp.maximum(z - 1, 0))), z > 0)
        else:
            target = 3 - z if i == 1 else 3 * (z // 2)
            relay = remote(own, own, zsnd.at[3], bzrcv.at[k, zp], at_z(target))
            relay.wait_recv()
            send(relay, inner)

    def down_project(k):
        depth = ff // 4
        for n in range(4):
            g = G[k, :, :, :, n * depth:(n + 1) * depth].reshape(NY * NZ * ROWS, depth)
            part = jnp.dot(g, W[n * depth:(n + 1) * depth, :], preferred_element_type=F32)
            if n == 0:
                acc[...] = part
            elif n < 3:
                acc[...] += part
            else:
                Pb[k] = (acc[...] + part).astype(BF).reshape(NY, NZ, ROWS, feats)
        for j in range(1, ND):
            dd = (d + j) % ND
            send(remote(Pb.at[k, pl.ds(2 * (dd % 2), 2), dd // 2], R.at[k, j - 1], osnd.at[4], drcv.at[k], at_d(dd)))

    def boundary(k):
        total = res[:, k].astype(F32) + Pb[k, pl.ds(2 * (d % 2), 2), d // 2].astype(F32)
        drain(R.at[k], drcv.at[k])
        for j in range(ND - 1):
            total = total + R[k, j].astype(F32)
        B[k] = total.astype(BF)
        send(remote(B.at[k], E.at[k, d // 2, d % 2], osnd.at[5], srcv.at[k], ((s + 1) % NS, d, t)))

    def spread(k):
        own = E.at[k, d // 2, d % 2]
        drain(own, srcv.at[k])
        for j in range(1, ND):
            send(remote(own, own, osnd.at[6], grcv.at[k], at_d((d + j) % ND)))

    def project_pairs(k):
        drain(R.at[k], grcv.at[k])
        x = E[k].reshape(NY * NZ * ROWS, feats).astype(F32)
        scaled = (x * gain[...]).astype(BF)
        XS[k] = scaled
        UK[k] = jnp.dot(scaled, WP[:, 512:768], preferred_element_type=F32).astype(BF).reshape(NZ, 2, 2, ROWS, 256)
        SQ[k] = lax.dot_general(
            jnp.ones((8, feats), BF), (x * x).astype(BF), (((1,), (1,)), ((), ())), preferred_element_type=F32
        )
        for j in range(1, NY):
            yy = (y + j) % NY
            send(remote(UK.at[k, :, yy // 2, yy % 2], RK.at[k, j - 1], osnd.at[7], ukrcv.at[k], at_y(yy)))
            send(remote(SQ.at[k], SY.at[k, j - 1], osnd.at[8], qyrcv.at[k], at_y(yy)))

    def project_queries(k):
        UQ[k] = jnp.dot(XS[k], WP[:, 0:512], preferred_element_type=F32).astype(BF).reshape(NZ, 2, 2, ROWS, 512)
        for j in range(1, NY):
            yy = (y + j) % NY
            send(remote(UQ.at[k, :, yy // 2, yy % 2], RQ.at[k, j - 1], osnd.at[9], uqrcv.at[k], at_y(yy)))

    def sum_pairs_y(k):
        drain(RK.at[k], ukrcv.at[k])
        drain(SY.at[k], qyrcv.at[k])
        total = UK[k, :, y // 2, y % 2].astype(F32)
        squares = SQ[k]
        for j in range(1, NY):
            total = total + RK[k, j - 1].astype(F32)
            squares = squares + SY[k, j - 1]
        VK[k] = total.astype(BF)
        SV[k] = squares
        for j in range(1, NZ):
            zz = (z + j) % NZ
            send(remote(VK.at[k, zz], ZK.at[k, j - 1], osnd.at[10], vkrcv.at[k], at_z(zz)))
            send(remote(SV.at[k], SZ.at[k, j - 1], osnd.at[11], qzrcv.at[k], at_z(zz)))

    def sum_queries_y(k):
        drain(RQ.at[k], uqrcv.at[k])
        total = UQ[k, :, y // 2, y % 2].astype(F32)
        for j in range(1, NY):
            total = total + RQ[k, j - 1].astype(F32)
        VQ[k] = total.astype(BF)
        for j in range(1, NZ):
            zz = (z + j) % NZ
            send(remote(VQ.at[k, zz], ZQ.at[k, j - 1], osnd.at[12], vqrcv.at[k], at_z(zz)))

    def rotate(u, k):
        rows = pl.ds(k * ROWS, ROWS)
        return (u * ctab[rows, :] + pltpu.roll(u, HD // 2, 1) * stab[rows, :]).astype(BF)

    def sum_pairs_z(k):
        drain(ZK.at[k], vkrcv.at[k])
        drain(SZ.at[k], qzrcv.at[k])
        total = VK[k, z].astype(F32)
        squares = SV[k]
        for j in range(1, NZ):
            total = total + ZK[k, j - 1].astype(F32)
            squares = squares + SZ[k, j - 1]
        tokens = NY * NZ * ROWS
        lane = lax.broadcasted_iota(jnp.int32, (ROWS, tokens), 1)
        row = lax.broadcasted_iota(jnp.int32, (ROWS, tokens), 0)
        row_squares = jnp.broadcast_to(squares[0:1, :], (ROWS, tokens))
        own_squares = jnp.sum(jnp.where(lane == row + t * ROWS, row_squares, 0.0), axis=1, keepdims=True)
        inverse = lax.rsqrt(own_squares / D + EPSILON)
        inv[k] = jnp.broadcast_to(inverse, (ROWS, HD))
        KV[k, y, z, :, 0:HD] = rotate(total[:, 0:HD] * inverse, k)
        KV[k, y, z, :, HD:2 * HD] = (total[:, HD:2 * HD] * inverse).astype(BF)
        own = KV.at[k, y, z]
        for j in range(1, NZ):
            send(remote(own, own, osnd.at[13], kzrcv.at[k], at_z((z + j) % NZ)))

    def sum_queries_z(k):
        drain(ZQ.at[k], vqrcv.at[k])
        total = VQ[k, z].astype(F32)
        for j in range(1, NZ):
            total = total + ZQ[k, j - 1].astype(F32)
        for h in range(4):
            Qb[h, k * ROWS:(k + 1) * ROWS, :] = rotate(total[:, h * HD:(h + 1) * HD] * inv[k], k)

    def pairs_y(k):
        drain(KV.at[k, y, pl.ds(0, NZ - 1)], kzrcv.at[k])
        own = KV.at[k, y]
        for j in range(1, NY):
            send(remote(own, own, osnd.at[14], kyrcv.at[k], at_y((y + j) % NY)))

    def pairs_end(k):
        drain(KV.at[k, pl.ds(0, NY - 1)], kyrcv.at[k])

    def attend(first, last):
        tokens = (last - first) * NY * NZ * ROWS
        queries = Qb[...].reshape(4 * 64, HD)
        keys = KV[first:last, :, :, :, 0:HD].reshape(tokens, HD)
        values = KV[first:last, :, :, :, HD:2 * HD].reshape(tokens, HD)
        scores = lax.dot_general(queries, keys, (((1,), (1,)), ((), ())), preferred_element_type=F32) * HD ** (-0.5)
        lane = lax.broadcasted_iota(jnp.int32, (1, tokens), 1) + first * NY * NZ * ROWS
        key_at = ((lane >> 4) & 3) * 256 + ((lane >> 6) & 3) * 64 + (lane >> 8) * 16 + (lane & 15)
        row = lax.broadcasted_iota(jnp.int32, (256, 1), 0)
        query_at = (row & 63) + t * 64
        scores = jnp.where(key_at <= query_at, scores, -1e30)
        top = jnp.max(scores, axis=1, keepdims=True)
        if first > 0:
            top = jnp.maximum(top, peak[...])
        weights = jnp.exp(scores - top)
        total = jnp.sum(weights, axis=1, keepdims=True)
        result = jnp.dot(weights.astype(BF), values, preferred_element_type=F32)
        if first > 0:
            fade = jnp.exp(peak[...] - top)
            total = total + mass[...] * fade
            result = result + mixed[...] * fade
        if last < NK:
            peak[...] = top
            mass[...] = total
            mixed[...] = result
        else:
            result = (result / total).astype(BF)
            for h in range(4):
                out[:, h * HD:(h + 1) * HD] = result[h * 64:(h + 1) * 64, :]

    def gathered():
        @pl.when(inner)
        def _():
            drain(G.at[:, 0, pl.ds(0, 2), :, near], zsnd.at[0])
            drain(G.at[:, 0, pl.ds(0, 3), :, near], zsnd.at[1])
            drain(G.at[:, pl.ds(0, 2), :, :, later], zsnd.at[2])
            drain(G.at[:, pl.ds(0, 3), :, :, later], zsnd.at[3])

        @pl.when(jnp.logical_not(inner))
        def _():
            drain(G.at[:, 0, 0, :, near], zsnd.at[0])
            drain(G.at[:, 0, :, :, later], zsnd.at[2])

        drain(G.at[:, pl.ds(0, 2), :, :, near], osnd.at[0])
        drain(G.at[:, 0, :, :, near], osnd.at[1])
        drain(G.at[:, 0, pl.ds(0, 2), :, later], osnd.at[2])
        drain(G.at[:, 0, 0, :, later], osnd.at[3])

    def left():
        drain(R, osnd.at[4])
        drain(B, osnd.at[5])
        drain(R, osnd.at[6])
        for at, ref in enumerate((RK, SY, RQ, ZK, SZ, ZQ)):
            drain(ref, osnd.at[7 + at])
        drain(KV.at[:, 0, pl.ds(0, NZ - 1)], osnd.at[13])

    steps = dict(
        gz=gather_z, gy=gather_y, ge=gather_end, ry=rest_y, rf=rest_far, rz=rest_z, dp=down_project, bd=boundary,
        sp=spread, pp=project_pairs, pq=project_queries, ky=sum_pairs_y, qy=sum_queries_y, kz=sum_pairs_z,
        qz=sum_queries_z, py=pairs_y, pe=pairs_end, at=attend,
    )
    for at, (name, *which) in enumerate(ORDER):
        if at == LOADED:
            for copy in local[1:]:
                copy.wait()
        if at == GATHERED:
            gathered()
        if at == LEFT:
            left()
        steps[name](*which)
    drain(KV.at[:, pl.ds(0, NY - 1)], osnd.at[14])


def per_device(hidden, down_weight, residual, norm_gain, query_weight, key_value_weight):
    own_rows, ff = hidden.shape[1:]
    feats = down_weight.shape[2]
    positions = (lax.axis_index("tensor") * own_rows + jnp.arange(own_rows, dtype=jnp.int32)).astype(F32)
    frequency = ROPE_BASE ** (-jnp.arange(HD // 2, dtype=F32) * 2.0 / HD)
    angles = positions[:, None] * frequency[None, :]
    cosine, sine = jnp.cos(angles), jnp.sin(angles)
    ctab = jnp.concatenate([cosine, cosine], axis=1)
    stab = jnp.concatenate([-sine, sine], axis=1)
    chunk = NY * NZ * ROWS
    dma = pltpu.SemaphoreType.DMA
    vmem = pl.BlockSpec(memory_space=pltpu.VMEM)
    hbm = pl.BlockSpec(memory_space=pltpu.HBM)
    attended = pl.pallas_call(
        kernel,
        out_shape=jax.ShapeDtypeStruct((own_rows, 512), BF),
        in_specs=[hbm] * 8,
        out_specs=vmem,
        scratch_shapes=[
            pltpu.VMEM((2, NK, ROWS, feats), BF),
            pltpu.VMEM((1, feats), F32),
            pltpu.VMEM((own_rows, HD), F32),
            pltpu.VMEM((own_rows, HD), F32),
            pltpu.VMEM((4 * own_rows, 1), F32),
            pltpu.VMEM((4 * own_rows, 1), F32),
            pltpu.VMEM((4 * own_rows, HD), F32),
            pltpu.VMEM((NK, NY, NZ, ROWS, ff), BF),
            pltpu.VMEM((ff, feats), BF),
            pltpu.VMEM((feats, 768), BF),
            pltpu.VMEM((chunk, feats), F32),
            pltpu.VMEM((NK, NY, NZ, ROWS, feats), BF),
            pltpu.VMEM((NK, ND - 1, 2, ROWS, feats), BF),
            pltpu.VMEM((NK, 2, ROWS, feats), BF),
            pltpu.VMEM((NK, NZ, 2, 2, ROWS, feats), BF),
            pltpu.VMEM((NK, chunk, feats), BF),
            pltpu.VMEM((NK, NZ, 2, 2, ROWS, 256), BF),
            pltpu.VMEM((NK, NZ, 2, 2, ROWS, 512), BF),
            pltpu.VMEM((NK, NY - 1, NZ, ROWS, 256), BF),
            pltpu.VMEM((NK, NY - 1, NZ, ROWS, 512), BF),
            pltpu.VMEM((NK, NZ, ROWS, 256), BF),
            pltpu.VMEM((NK, NZ, ROWS, 512), BF),
            pltpu.VMEM((NK, NZ - 1, ROWS, 256), BF),
            pltpu.VMEM((NK, NZ - 1, ROWS, 512), BF),
            pltpu.VMEM((NK, 8, chunk), F32),
            pltpu.VMEM((NK, NY - 1, 8, chunk), F32),
            pltpu.VMEM((NK, 8, chunk), F32),
            pltpu.VMEM((NK, NZ - 1, 8, chunk), F32),
            pltpu.VMEM((NK, ROWS, HD), F32),
            pltpu.VMEM((4, own_rows, HD), BF),
            pltpu.VMEM((NK, NY, NZ, ROWS, 2 * HD), BF),
            dma((8,)),
            dma((4,)),
            dma((15,)),
            dma((NK, NZ)), dma((NK, NZ, 2)), dma((NK,)), dma((NK, 2)), dma((NK,)), dma((NK, NZ)),
            dma((NK,)), dma((NK,)), dma((NK,)), dma((NK,)), dma((NK,)), dma((NK,)),
            dma((NK,)), dma((NK,)), dma((NK,)), dma((NK,)), dma((NK,)),
        ],
        compiler_params=pltpu.CompilerParams(collective_id=0, has_side_effects=True, vmem_limit_bytes=62 << 20),
    )(
        hidden.reshape(NK, ROWS, ff),
        down_weight[0],
        query_weight[0],
        key_value_weight[0],
        residual.reshape(2, NK, ROWS, feats),
        norm_gain,
        ctab,
        stab,
    )
    return attended[None]


def solution(mesh):
    placed = (
        P("section", "tensor", "dp"),
        P("section", "dp", "tensor"),
        P("section", "dp", "tensor"),
        P("section", "tensor"),
        P("section", "tensor", "dp"),
        P("section", "tensor", "dp"),
    )
    return jax.shard_map(
        per_device,
        mesh=mesh,
        in_specs=placed,
        out_specs=P("section", "tensor", "dp"),
        check_vma=False,
    )
```

time: 119 us -> 112 us (0.941)
  Pallas kernels: 115 us -> 109 us
    pallas_call x1, Pallas kernels: 115 us -> 109 us  [per_device(): pl.pallas_call(kernel, out_shape=jax.ShapeDtypeStruct((own_rows, 512), BF...]
where the time goes in v3:
time: 112 us; the launch traced here: 111 us
  Pallas kernels  109 us (97%)
  local copies, waits for them, and re-layouts  1.47 us (1%)
    pallas_call x1, Pallas kernels, per_device(): pl.pallas_call(kernel, out_shape=jax.ShapeDtypeStruct((own_rows, 512), BF...  109 us

profile of v3, /device:TPU:6, one launch (start us, length us, event | category | flops | bytes accessed | tf_op | source)
XLA Modules:
  0.0 110.9 jit_solution(18372294355059633376)
XLA Ops:
  0.0 0.2 fusion
  0.2 0.7 pad_maximum_fusion
  0.9 108.5 %shard_map.64 = bf16[64,512]{1,0:T(8,128)(2,1)} custom-call(bf16[4,16,3584]{2,1,0:T(8,128)(2,1)} %bitcast.8, bf16[3584,512]{1,0:T(8,128)(2,1)} %bitcast.6, bf16[512,512]{1,0:T(8,128)(2,1)} %bitcast.7, bf16[512,256]{1,0:T(8,128)(2,1)} %bitcast.10, bf16[2,4,16,512]{3,2,1,0:T(8,128)(2,1)} %bitcast.11, f32[1,512]{1,0:T(1,128)} %gain_hbm.1, ...), custom_call_target="tpu_custom_call" | custom-call | tf_op jit(solution)/shard_map/pallas_call | solution.py:366
  109.5 1.5 %copy.8 = bf16[1,64,512]{2,1,0:T(8,128)(2,1)} copy(bf16[1,64,512]{2,1,0:T(8,128)(2,1)} %bitcast.9) | data formatting | bytes 131072
  (2 shorter events, 0.0 us)

commit v4 on v3

--- a/solution.py
+++ b/solution.py
@@ -20,19 +20,19 @@
 
 COLS = 24
 ORDER = [
-    ("ry", 1), ("ry", 0), ("ry", 3), ("gz", 0, 0), ("gz", 1, 0), ("rf", 3), ("rf", 1), ("rf", 0),
-    ("ry", 2), ("gz", 0, 1), ("gz", 1, 1), ("gz", 2, 0), ("gz", 0, 2), ("rz", 1, 0), ("rz", 0, 0), ("gy", 0, 0),
-    ("rf", 2), ("gz", 0, 3), ("gy", 2, 0), ("gz", 2, 1), ("gy", 0, 1), ("rz", 1, 1), ("gz", 1, 2), ("gy", 0, 2),
-    ("rz", 2, 0), ("gy", 1, 0), ("gz", 1, 3), ("rz", 0, 1), ("gy", 0, 3), ("rz", 0, 2), ("rz", 3, 0), ("gz", 3, 0),
-    ("gz", 2, 2), ("rz", 0, 3), ("gz", 2, 3), ("rz", 1, 2), ("rz", 2, 1), ("gy", 1, 1), ("rz", 1, 3), ("ge", 0),
-    ("dp", 0), ("gy", 1, 2), ("rz", 2, 2), ("gy", 1, 3), ("rz", 3, 1), ("gy", 2, 1), ("gz", 3, 1), ("rz", 3, 2),
-    ("gy", 2, 2), ("bd", 0), ("gy", 2, 3), ("gz", 3, 2), ("ge", 1), ("rz", 2, 3), ("dp", 1), ("gy", 3, 0),
-    ("gz", 3, 3), ("sp", 0), ("gy", 3, 1), ("ge", 2), ("bd", 1), ("dp", 2), ("rz", 3, 3), ("gy", 3, 2),
-    ("gy", 3, 3), ("sp", 1), ("bd", 2), ("ge", 3), ("dp", 3), ("pp", 0), ("pq", 0), ("sp", 2),
-    ("pp", 1), ("pq", 1), ("bd", 3), ("pp", 2), ("pq", 2), ("sp", 3), ("ky", 1), ("ky", 0),
-    ("qy", 1), ("pp", 3), ("ky", 2), ("pq", 3), ("kz", 0), ("qy", 0), ("ky", 3), ("kz", 2),
-    ("kz", 1), ("py", 0), ("qy", 2), ("qz", 0), ("qz", 1), ("kz", 3), ("py", 2), ("qy", 3),
-    ("py", 1), ("py", 3), ("qz", 2), ("pe", 2), ("pe", 0), ("pe", 1), ("qz", 3), ("at", 0, 2),
+    ("ry", 3), ("ry", 0), ("ry", 1), ("ry", 2), ("gz", 0, 0), ("rf", 1), ("rf", 3), ("gz", 1, 0),
+    ("gz", 0, 1), ("rf", 0), ("gz", 2, 0), ("gz", 2, 1), ("rz", 0, 0), ("gz", 1, 1), ("gz", 0, 2), ("gz", 0, 3),
+    ("rz", 0, 1), ("rf", 2), ("gz", 2, 2), ("gy", 0, 0), ("gy", 0, 1), ("rz", 1, 0), ("rz", 0, 2), ("gz", 2, 3),
+    ("rz", 2, 0), ("rz", 1, 1), ("rz", 0, 3), ("gy", 2, 0), ("gy", 2, 1), ("gy", 0, 2), ("gy", 0, 3), ("rz", 1, 2),
+    ("gz", 1, 2), ("rz", 3, 0), ("rz", 2, 1), ("gz", 3, 0), ("gy", 2, 2), ("ge", 0), ("gy", 2, 3), ("dp", 0),
+    ("gz", 1, 3), ("rz", 3, 1), ("gy", 1, 0), ("gy", 1, 1), ("rz", 1, 3), ("gy", 1, 2), ("gz", 3, 1), ("rz", 2, 2),
+    ("rz", 2, 3), ("ge", 2), ("bd", 0), ("dp", 2), ("gy", 1, 3), ("gz", 3, 2), ("gz", 3, 3), ("sp", 0),
+    ("gy", 3, 0), ("bd", 2), ("gy", 3, 1), ("ge", 1), ("dp", 1), ("rz", 3, 2), ("rz", 3, 3), ("gy", 3, 2),
+    ("gy", 3, 3), ("pp", 0), ("sp", 2), ("bd", 1), ("ge", 3), ("dp", 3), ("pq", 0), ("sp", 1),
+    ("pp", 2), ("bd", 3), ("pq", 2), ("pp", 1), ("ky", 0), ("ky", 2), ("pq", 1), ("sp", 3),
+    ("qy", 2), ("qy", 0), ("ky", 1), ("kz", 0), ("qy", 1), ("kz", 2), ("pp", 3), ("pq", 3),
+    ("py", 0), ("kz", 1), ("ky", 3), ("py", 2), ("pe", 0), ("qy", 3), ("py", 1), ("kz", 3),
+    ("py", 3), ("qz", 1), ("pe", 1), ("qz", 0), ("qz", 2), ("qz", 3), ("at", 0, 2), ("pe", 2),
     ("at", 2, 3), ("pe", 3), ("at", 3, 4),
 ]
 LOADED = min(ORDER.index(("dp", k)) for k in range(NK))
@@ -196,9 +196,11 @@
         scaled = (x * gain[...]).astype(BF)
         XS[k] = scaled
         UK[k] = jnp.dot(scaled, WP[:, 512:768], preferred_element_type=F32).astype(BF).reshape(NZ, 2, 2, ROWS, 256)
-        SQ[k] = lax.dot_general(
+        squares = lax.dot_general(
             jnp.ones((8, feats), BF), (x * x).astype(BF), (((1,), (1,)), ((), ())), preferred_element_type=F32
         )
+        lower = lax.broadcasted_iota(jnp.int32, (8, HD), 0) == 0
+        SQ[k] = jnp.where(lower, squares[:, 0:HD], squares[:, HD:2 * HD])
         for j in range(1, NY):
             yy = (y + j) % NY
             send(remote(UK.at[k, :, yy // 2, yy % 2], RK.at[k, j - 1], osnd.at[7], ukrcv.at[k], at_y(yy)))
@@ -250,15 +252,17 @@
         tokens = NY * NZ * ROWS
         lane = lax.broadcasted_iota(jnp.int32, (ROWS, tokens), 1)
         row = lax.broadcasted_iota(jnp.int32, (ROWS, tokens), 0)
-        row_squares = jnp.broadcast_to(squares[0:1, :], (ROWS, tokens))
+        row_squares = jnp.concatenate(
+            [jnp.broadcast_to(squares[0:1, :], (ROWS, HD)), jnp.broadcast_to(squares[1:2, :], (ROWS, HD))], axis=1
+        )
         own_squares = jnp.sum(jnp.where(lane == row + t * ROWS, row_squares, 0.0), axis=1, keepdims=True)
         inverse = lax.rsqrt(own_squares / D + EPSILON)
         inv[k] = jnp.broadcast_to(inverse, (ROWS, HD))
         KV[k, y, z, :, 0:HD] = rotate(total[:, 0:HD] * inverse, k)
         KV[k, y, z, :, HD:2 * HD] = (total[:, HD:2 * HD] * inverse).astype(BF)
         own = KV.at[k, y, z]
-        for j in range(1, NZ):
-            send(remote(own, own, osnd.at[13], kzrcv.at[k], at_z((z + j) % NZ)))
+        for j in range(1, NY):
+            send(remote(own, own, osnd.at[13], kyrcv.at[k], at_y((y + j) % NY)))
 
     def sum_queries_z(k):
         drain(ZQ.at[k], vqrcv.at[k])
@@ -268,14 +272,14 @@
         for h in range(4):
             Qb[h, k * ROWS:(k + 1) * ROWS, :] = rotate(total[:, h * HD:(h + 1) * HD] * inv[k], k)
 
-    def pairs_y(k):
-        drain(KV.at[k, y, pl.ds(0, NZ - 1)], kzrcv.at[k])
-        own = KV.at[k, y]
-        for j in range(1, NY):
-            send(remote(own, own, osnd.at[14], kyrcv.at[k], at_y((y + j) % NY)))
+    def pairs_z(k):
+        drain(KV.at[k, pl.ds(0, NY - 1), z], kyrcv.at[k])
+        own = KV.at[k, :, z]
+        for j in range(1, NZ):
+            send(remote(own, own, osnd.at[14], kzrcv.at[k], at_z((z + j) % NZ)))
 
     def pairs_end(k):
-        drain(KV.at[k, pl.ds(0, NY - 1)], kyrcv.at[k])
+        drain(KV.at[k, :, pl.ds(0, NZ - 1)], kzrcv.at[k])
 
     def attend(first, last):
         tokens = (last - first) * NY * NZ * ROWS
@@ -331,12 +335,12 @@
         drain(R, osnd.at[6])
         for at, ref in enumerate((RK, SY, RQ, ZK, SZ, ZQ)):
             drain(ref, osnd.at[7 + at])
-        drain(KV.at[:, 0, pl.ds(0, NZ - 1)], osnd.at[13])
+        drain(KV.at[:, pl.ds(0, NY - 1), 0], osnd.at[13])
 
     steps = dict(
         gz=gather_z, gy=gather_y, ge=gather_end, ry=rest_y, rf=rest_far, rz=rest_z, dp=down_project, bd=boundary,
         sp=spread, pp=project_pairs, pq=project_queries, ky=sum_pairs_y, qy=sum_queries_y, kz=sum_pairs_z,
-        qz=sum_queries_z, py=pairs_y, pe=pairs_end, at=attend,
+        qz=sum_queries_z, py=pairs_z, pe=pairs_end, at=attend,
     )
     for at, (name, *which) in enumerate(ORDER):
         if at == LOADED:
@@ -347,7 +351,7 @@
         if at == LEFT:
             left()
         steps[name](*which)
-    drain(KV.at[:, pl.ds(0, NY - 1)], osnd.at[14])
+    drain(KV.at[:, :, pl.ds(0, NZ - 1)], osnd.at[14])
 
 
 def per_device(hidden, down_weight, residual, norm_gain, query_weight, key_value_weight):
@@ -393,10 +397,10 @@
             pltpu.VMEM((NK, NZ, ROWS, 512), BF),
             pltpu.VMEM((NK, NZ - 1, ROWS, 256), BF),
             pltpu.VMEM((NK, NZ - 1, ROWS, 512), BF),
-            pltpu.VMEM((NK, 8, chunk), F32),
-            pltpu.VMEM((NK, NY - 1, 8, chunk), F32),
-            pltpu.VMEM((NK, 8, chunk), F32),
-            pltpu.VMEM((NK, NZ - 1, 8, chunk), F32),
+            pltpu.VMEM((NK, 8, chunk // 2), F32),
+            pltpu.VMEM((NK, NY - 1, 8, chunk // 2), F32),
+            pltpu.VMEM((NK, 8, chunk // 2), F32),
+            pltpu.VMEM((NK, NZ - 1, 8, chunk // 2), F32),
             pltpu.VMEM((NK, ROWS, HD), F32),
             pltpu.VMEM((4, own_rows, HD), BF),
             pltpu.VMEM((NK, NY, NZ, ROWS, 2 * HD), BF),

time: 112 us -> 111 us (level)
  no operation moved by 1% of the time
where the time goes in v4:
time: 111 us; the launch traced here: 110 us
  Pallas kernels  108 us (97%)
  local copies, waits for them, and re-layouts  1.47 us (1%)
    pallas_call x1, Pallas kernels, per_device(): pl.pallas_call(kernel, out_shape=jax.ShapeDtypeStruct((own_rows, 512), BF...  108 us

profile of v4, /device:TPU:6, one launch (start us, length us, event | category | flops | bytes accessed | tf_op | source)
XLA Modules:
  0.0 110.1 jit_solution(14016935480712072291)
XLA Ops:
  0.0 0.2 fusion
  0.2 0.7 pad_maximum_fusion
  0.9 107.7 %shard_map.64 = bf16[64,512]{1,0:T(8,128)(2,1)} custom-call(bf16[4,16,3584]{2,1,0:T(8,128)(2,1)} %bitcast.8, bf16[3584,512]{1,0:T(8,128)(2,1)} %bitcast.6, bf16[512,512]{1,0:T(8,128)(2,1)} %bitcast.7, bf16[512,256]{1,0:T(8,128)(2,1)} %bitcast.10, bf16[2,4,16,512]{3,2,1,0:T(8,128)(2,1)} %bitcast.11, f32[1,512]{1,0:T(1,128)} %gain_hbm.1, ...), custom_call_target="tpu_custom_call" | custom-call | tf_op jit(solution)/shard_map/pallas_call | solution.py:370
  108.6 1.5 %copy.8 = bf16[1,64,512]{2,1,0:T(8,128)(2,1)} copy(bf16[1,64,512]{2,1,0:T(8,128)(2,1)} %bitcast.9) | data formatting | bytes 131072
  (2 shorter events, 0.0 us)
